TPU v7x, 128 devices: a whole 4x4x4 slice. The times are simulated.
128 devices in a mesh: mat: 8 (over z, core), pts: 16 (over y, x).
Axes of the slice: x: 4, y: 4, z: 4, core: 2. Of those that a mesh axis runs over, the one named last changes fastest.
Arguments:
- basis_values: bfloat16 [512, 2048, 512], P(('mat', 'pts')), may hold values from -6 to 6
- tile_ids: int32 [512, 4], P(('mat', 'pts')), may hold values from 0 to 7, as said below
- density_matrix: bfloat16 [1024, 1024], P('mat'), may hold values from -0.01171875 to 0.01171875
- descriptors: bfloat16 [512, 2048, 64], P(('mat', 'pts')), may hold values from -6 to 6
- grid_weights: float32 [512, 2048], P(('mat', 'pts')), may hold values from 0.25 to 2
- centre_ids: int32 [512, 2048], P(('mat', 'pts')), may hold values from 0 to 255
- density_scale: float32 [64], replicated, may hold values from -4 to 4
- norm_gain: float32 [64], replicated, may hold values from 0.1 to 1.9
- w_first: bfloat16 [64, 256], replicated, may hold values from -0.75 to 0.75
- b_first: float32 [256], replicated, may hold values from -3 to 3
- w_second: bfloat16 [256, 256], replicated, may hold values from -0.375 to 0.375
- b_second: float32 [256], replicated, may hold values from -3 to 3
- w_third: bfloat16 [256, 64], replicated, may hold values from -0.375 to 0.375
- b_third: float32 [64], replicated, may hold values from -3 to 3
Outputs:
- potential_matrix: bfloat16 [1024, 1024], P('mat', 'pts')
- centre_features: bfloat16 [256, 64], P('pts')
Inputs may be any that keep to these rules, and one draw needn't show every extreme that they name: `tile_ids`: the 4 tiles t of one batch have 4 different values of t.
All inputs are finite; a program needn't handle non-finite values.
Results may differ from a plain program's by a relative error of at most 0.0064.
Values may be sent and summed in bfloat16 or wider, within the bound.
No kernel may reach another device: no remote copies, remote signals or barrier semaphores. Data moves between devices by JAX's collectives and lax.ppermute only.
A program may use at most 64 MiB of HBM per device.

v0:
```python
import math

import jax
import jax.numpy as jnp
from jax import lax
from jax.sharding import PartitionSpec as P

CENT_DEV = 16


def laid_out(parts, dim):
    shape = list(parts.shape[1:])
    shape[dim] *= parts.shape[0]
    return jnp.moveaxis(parts, 0, dim).reshape(shape)


def sent_to_all(value, axis):
    copies = jnp.broadcast_to(value, (lax.axis_size(axis), *value.shape))
    return lax.all_to_all(copies, axis, split_axis=0, concat_axis=0, tiled=True)


def gather_directly(value, axis, dim):
    return laid_out(sent_to_all(value, axis), dim)


def cut_along(value, dim, peers):
    shape = value.shape
    parts = value.reshape(*shape[:dim], peers, shape[dim] // peers, *shape[dim + 1 :])
    return jnp.moveaxis(parts, dim, 0)


def summed_on_arrival(value, axis, dim):
    peers = lax.axis_size(axis)
    parts = lax.all_to_all(cut_along(value, dim, peers), axis, 0, 0, tiled=True)
    return jnp.sum(parts, axis=0)


def taken_together(value, axis):
    return sent_to_all(value, axis).sum(axis=0)


def centre_network(summed, norm_gain, w_first, b_first, w_second, b_second, w_third, b_third):
    inverse = lax.rsqrt(jnp.mean(summed * summed, axis=1, keepdims=True) + 1e-05)
    normed = (summed * inverse * norm_gain).astype(jnp.bfloat16)
    hidden_one = jax.nn.silu(
        jnp.dot(normed, w_first, preferred_element_type=jnp.float32) + b_first
    ).astype(jnp.bfloat16)
    hidden_two = jax.nn.silu(
        jnp.dot(hidden_one, w_second, preferred_element_type=jnp.float32) + b_second
    ).astype(jnp.bfloat16)
    return (jnp.dot(hidden_two, w_third, preferred_element_type=jnp.float32) + b_third).astype(
        jnp.bfloat16
    )


def shards(
    basis_values,
    tile_ids,
    density_matrix,
    descriptors,
    grid_weights,
    centre_ids,
    density_scale,
    norm_gain,
    w_first,
    b_first,
    w_second,
    b_second,
    w_third,
    b_third,
):
    batch_count, point_count, orbitals = basis_values.shape
    per_batch = tile_ids.shape[1]
    tile_size = orbitals // per_batch
    rows_dev, basis_count = density_matrix.shape
    tile_count = basis_count // tile_size
    feat_width = descriptors.shape[2]
    groups = lax.axis_size("mat")
    blank = jnp.zeros((batch_count, per_batch, tile_size, orbitals), jnp.bfloat16)
    portion = gather_directly(density_matrix, "mat", 0)
    tiles_here = portion.shape[0] // tile_size
    tiled = portion.reshape(tiles_here, tile_size, tile_count, tile_size)
    inside = (tile_ids >= 0) & (tile_ids < tiles_here)
    clipped = jnp.clip(tile_ids, 0, tiles_here - 1)
    chosen = tiled[clipped[:, :, None], :, tile_ids[:, None, :]]
    chosen = chosen.transpose(0, 1, 3, 2, 4).reshape(batch_count, per_batch, tile_size, orbitals)
    panels = jnp.where(inside[:, :, None, None], chosen, blank)
    panel_full = panels.reshape(batch_count, orbitals, orbitals)
    projected = jnp.einsum(
        "bpa,bac->bpc", basis_values, panel_full, preferred_element_type=jnp.float32
    )
    density = jnp.sum(basis_values.astype(jnp.float32) * projected, axis=2)
    radial_terms = descriptors.astype(jnp.float32)
    features = jax.nn.silu(density[:, :, None] * density_scale + radial_terms)
    weighted_feat = grid_weights[:, :, None] * features
    centre_count = CENT_DEV * lax.axis_size("pts")
    partial_value = jax.ops.segment_sum(
        weighted_feat.reshape(-1, feat_width), centre_ids.reshape(-1), num_segments=centre_count
    )
    summed = summed_on_arrival(partial_value, "pts", 0)
    total_sum = taken_together(summed, "mat")
    centre_features = centre_network(
        total_sum, norm_gain, w_first, b_first, w_second, b_second, w_third, b_third
    )
    everyone = gather_directly(centre_features, "pts", 0)
    nearest = everyone[centre_ids].astype(jnp.float32)
    batches_all = batch_count * groups * lax.axis_size("pts")
    factor = tile_count / (per_batch * math.sqrt(point_count * feat_width * batches_all))
    point_potential = grid_weights * density * jnp.sum(nearest * radial_terms, axis=2) * factor
    weighted = (point_potential[:, :, None] * basis_values.astype(jnp.float32)).astype(jnp.bfloat16)
    blocks_out = jnp.einsum(
        "bpa,bpc->bac", basis_values, weighted, preferred_element_type=jnp.float32
    )
    tile_blocks = blocks_out.reshape(
        batch_count, per_batch, tile_size, per_batch, tile_size
    ).transpose(0, 1, 3, 2, 4)
    whole = jnp.zeros((tile_count, tile_size, tile_count, tile_size), jnp.float32)
    whole = whole.at[tile_ids[:, :, None], :, tile_ids[:, None, :]].add(tile_blocks)
    row_part = lax.psum_scatter(
        whole.reshape(basis_count, basis_count), "mat", scatter_dimension=0, tiled=True
    )
    potential_matrix = summed_on_arrival(row_part, "pts", 1).astype(jnp.bfloat16)
    return (potential_matrix, centre_features)


def solution(mesh):
    return jax.shard_map(
        shards,
        mesh=mesh,
        in_specs=(
            P(("mat", "pts"), None, None),
            P(("mat", "pts"), None),
            P("mat", None),
            P(("mat", "pts"), None, None),
            P(("mat", "pts"), None),
            P(("mat", "pts"), None),
            P(),
            P(),
            P(),
            P(),
            P(),
            P(),
            P(),
            P(),
        ),
        out_specs=(P("mat", "pts"), P("pts", None)),
        check_vma=False,
    )
```

profile of v0, /device:TPU:0, one launch (start us, length us, event | category | flops | bytes accessed | tf_op | source)
XLA Modules:
  0.0 283.6 jit_solution(4132089859656534719)
XLA Ops:
  7.2 0.0 copy-start
  7.2 0.0 copy-start.7
  7.2 1.2 copy.37
  8.4 1.7 broadcast_in_dim.38
  10.0 5.4 %all-to-all-start = ((bf16[8,128,1024]{1,2,0:T(8,128)(2,1)}), bf16[8,128,1024]{1,2,0:T(8,128)(2,1)S(1)}, u32[]{:S(2)}, u32[]{:S(2)}) async-start(bf16[8,128,1024]{1,2,0:T(8,128)(2,1)} %broadcast_in_dim.38), calls=%async_computation | async-start | bytes 4194304 | tf_op jit(solution)/shard_map/all_to_all | solution.py:19
  15.5 0.1 broadcast_or_fusion
  15.5 0.1 reshape.70
  15.6 0.0 copy-start.4
  15.7 11.5 %copy.36 = bf16[4,2048,512]{1,2,0:T(8,128)(2,1)} copy(bf16[4,2048,512]{2,1,0:T(8,128)(2,1)} %param.14) | data formatting | bytes 16777216 | tf_op args[0]
  27.2 0.1 broadcast_bitcast_fusion
  27.3 15.3 %all-to-all-done = bf16[8,128,1024]{1,2,0:T(8,128)(2,1)S(1)} async-done(((bf16[8,128,1024]{1,2,0:T(8,128)(2,1)}), bf16[8,128,1024]{1,2,0:T(8,128)(2,1)S(1)}, u32[]{:S(2)}, u32[]{:S(2)}) %all-to-all-start) | async-done | bytes 2097184 | tf_op jit(solution)/shard_map/all_to_all | solution.py:19
  42.6 2.6 copy.38
  45.3 2.5 gather_fusion
  47.8 3.1 %copy.39 = bf16[4,4,128,4,128]{4,3,2,1,0:T(4,128)(2,1)} copy(bf16[4,4,128,4,128]{4,2,3,1,0:T(8,128)(2,1)S(1)} %bitcast.52) | data formatting | bytes 4194304 | tf_op jit(solution)/shard_map/transpose | solution.py:86
  51.0 2.7 reshape.63
  53.7 0.0 copy-start.2
  53.7 0.0 copy-start.3
  53.7 0.0 copy-start.10
  53.7 9.0 %fusion = f32[4,2048]{1,0:T(4,128)S(1)} fusion(bf16[4,2048,512]{1,2,0:T(8,128)(2,1)} %copy.36, bf16[4,2048,512]{2,1,0:T(8,128)(2,1)} %param.14, bf16[4,512,512]{2,1,0:T(8,128)(2,1)S(1)} %reshape.63, pred[4,512]{1,0:T(4,128)(4,1)S(1)} %bitcast.59), kind=kOutput, calls=%fused_computation.6 | convolution fusion | flops 4308590592 | bytes 18909184 | tf_op jit(solution)/shard_map/bpa,bac->bpc/dot_general | solution.py:89
  62.7 0.0 copy-done.2
  62.7 0.7 multiply_multiply_fusion
  63.4 0.0 copy-start.11
  63.5 0.0 copy-start.12
  63.5 0.0 copy-start.13
  63.5 0.0 copy-start.5
  63.5 0.0 copy-start.8
  63.5 0.0 copy-start.9
  63.5 2.7 copy.48
  66.3 44.3 %scatter_custom_fusion = f32[256,64]{1,0:T(8,128)S(1)} fusion(s32[8192]{0:T(1024)S(1)} %bitcast.58, f32[8192,64]{1,0:T(8,128)} %bitcast.53, f32[]{:T(128)} %constant.10.clone.1), kind=kCustom, calls=%fused_computation.24 | custom fusion | flops 524288 | bytes 66048 | tf_op jit(solution)/shard_map/scatter-add | solution.py:97
  110.6 0.1 reshape.104
  110.7 14.5 %all_to_all.25 = f32[16,1,1024]{2,1,0:T(1,128)S(1)} all-to-all(f32[16,1,1024]{2,1,0:T(1,128)S(1)} %reshape.104), channel_id=1, replica_groups=mesh['mat'=8,'pts'=16] {'pts'}, dimensions={0} | all-to-all | bytes 131072 | tf_op jit(solution)/shard_map/all_to_all | solution.py:34
  125.2 0.5 broadcast.150
  125.8 0.8 reduce
  126.6 0.1 reshape.105
  126.7 0.7 reshape.106
  127.4 3.3 %all-to-all-start.2 = ((f32[8,1,1024]{2,1,0:T(1,128)}), f32[8,1,1024]{2,1,0:T(1,128)S(1)}, u32[]{:S(2)}, u32[]{:S(2)}) async-start(f32[8,1,1024]{2,1,0:T(1,128)} %reshape.106), calls=%async_computation.2 | async-start | bytes 65536 | tf_op jit(solution)/shard_map/all_to_all | solution.py:19
  130.7 5.3 %all-to-all-done.2 = f32[8,1,1024]{2,1,0:T(1,128)S(1)} async-done(((f32[8,1,1024]{2,1,0:T(1,128)}), f32[8,1,1024]{2,1,0:T(1,128)S(1)}, u32[]{:S(2)}, u32[]{:S(2)}) %all-to-all-start.2) | async-done | bytes 32800 | tf_op jit(solution)/shard_map/all_to_all | solution.py:19
  136.1 0.7 reduce.1
  136.8 0.1 reshape.107
  136.9 0.1 multiply_reduce_fusion
  137.1 0.2 multiply_convert_fusion.1
  137.3 0.3 fusion.11
  137.6 0.7 reshape.108
  138.3 3.5 %all-to-all-start.3 = ((bf16[16,2,512]{2,1,0:T(2,128)(2,1)}), bf16[16,2,512]{2,1,0:T(2,128)(2,1)S(1)}, u32[]{:S(2)}, u32[]{:S(2)}) async-start(bf16[16,2,512]{2,1,0:T(2,128)(2,1)} %reshape.108), calls=%async_computation.3 | async-start | bytes 65536 | tf_op jit(solution)/shard_map/all_to_all | solution.py:19
  141.8 0.2 reduce-scatter.2.cloned.1.call-start
  142.0 0.1 reshape.92
  142.1 7.2 %all-to-all-done.3 = bf16[16,2,512]{2,1,0:T(2,128)(2,1)S(1)} async-done(((bf16[16,2,512]{2,1,0:T(2,128)(2,1)}), bf16[16,2,512]{2,1,0:T(2,128)(2,1)S(1)}, u32[]{:S(2)}, u32[]{:S(2)}) %all-to-all-start.3) | async-done | bytes 32800 | tf_op jit(solution)/shard_map/all_to_all | solution.py:19
  149.3 0.1 reshape.109
  149.4 24.0 %gather_fusion.1 = bf16[8192,64]{1,0:T(8,128)(2,1)S(1)} fusion(bf16[256,64]{1,0:T(8,128)(2,1)S(1)} %bitcast.45, s32[8192]{0:T(1024)S(1)} %broadcast_clamp_fusion), kind=kCustom, calls=%fused_computation.1 | custom fusion | bytes 2129920 | tf_op jit(solution)/shard_map/gather | solution.py:106
  173.5 1.9 copy.43
  175.4 1.9 fusion.8
  177.3 12.2 %fusion.5 = f32[4,512,512]{1,2,0:T(8,128)} fusion(bf16[4,2048,512]{2,1,0:T(8,128)(2,1)} %param.14, bf16[4,2048,512]{1,2,0:T(8,128)(2,1)} %copy.36, f32[4,2048]{1,0:T(4,128)S(1)} %multiply_multiply_fusion.1), kind=kOutput, calls=%fused_computation.13 | convolution fusion | flops 4307550208 | bytes 21004288 | tf_op jit(solution)/shard_map/bpa,bpc->bac/dot_general | solution.py:111
  189.6 5.2 %reshape.67 = f32[4,4,128,4,128]{2,1,4,3,0:T(4,128)} reshape(f32[4,512,512]{1,2,0:T(8,128)} %fusion.5) | data formatting | bytes 8388608 | tf_op jit(solution)/shard_map/reshape | solution.py:114
  194.8 5.2 %copy.44 = f32[4,4,4,128,128]{4,3,2,1,0:T(8,128)} copy(f32[4,4,4,128,128]{3,1,4,2,0:T(4,128)} %bitcast.48) | data formatting | bytes 8388608 | tf_op jit(solution)/shard_map/transpose | solution.py:116
  200.0 2.5 broadcast_in_dim.32
  202.5 14.0 %scatter_fusion = f32[8,128,8,128]{3,1,2,0:T(8,128)} fusion(f32[8,128,8,128]{3,1,2,0:T(8,128)} %broadcast_in_dim.32, s32[64]{0:T(128)S(1)} %reshape.92, f32[64,128,128]{2,1,0:T(8,128)} %bitcast.46), kind=kCustom, calls=%fused_computation.3 | custom fusion | flops 1048576 | bytes 12583424 | tf_op jit(solution)/shard_map/scatter-add | solution.py:118
  216.6 4.6 %copy.45 = f32[8,128,8,128]{3,2,1,0:T(8,128)S(1)} copy(f32[8,128,8,128]{3,1,2,0:T(8,128)} %scatter_fusion) | data formatting | bytes 8388608 | tf_op jit(solution)/shard_map/scatter-add | solution.py:118
  221.1 0.0 copy-start.1
  221.1 2.9 %copy.56 = f32[128,8,8,128]{3,1,2,0:T(8,128)} copy(f32[128,8,8,128]{3,2,1,0:T(8,128)S(1)} %bitcast.49) | data formatting | bytes 8388608
  224.1 0.0 reduce-scatter.2.cloned.1.call-update
  224.1 34.2 %reduce-scatter.2.cloned.1.call-done = f32[128,1024]{1,0:T(8,128)} async-done(((f32[1024,1024]{1,0:T(8,128)}), f32[128,1024]{1,0:T(8,128)}) %reduce-scatter.2.cloned.1.call-update) | async-done | bytes 524304 | tf_op jit(solution)/shard_map/reduce_scatter | solution.py:119
  258.3 1.2 copy.46
  259.5 16.6 %all_to_all.26 = f32[16,128,64]{1,2,0:T(8,128)S(1)} all-to-all(f32[16,128,64]{1,2,0:T(8,128)S(1)} %bitcast.54), channel_id=1, replica_groups=mesh['mat'=8,'pts'=16] {'pts'}, dimensions={0} | all-to-all | bytes 1048576 | tf_op jit(solution)/shard_map/all_to_all | solution.py:34
  276.1 0.6 reduce_sum.59
  (27 shorter events, 0.2 us)
Async XLA Ops:
  7.2 130.1 %copy-start = (bf16[256,256]{1,0:T(8,128)(2,1)S(1)}, bf16[256,256]{1,0:T(8,128)(2,1)}, u32[]{:S(2)}) copy-start(bf16[256,256]{1,0:T(8,128)(2,1)} %param.24) | copy-start | bytes 393220
  7.2 8.2 %copy-start.7 = (s32[4,4]{1,0:T(4,128)S(1)}, s32[4,4]{1,0:T(4,128)}, u32[]{:S(2)}) copy-start(s32[4,4]{1,0:T(4,128)} %param.15) | copy-start | bytes 196
  10.0 32.6 %all-to-all-start = ((bf16[8,128,1024]{1,2,0:T(8,128)(2,1)}), bf16[8,128,1024]{1,2,0:T(8,128)(2,1)S(1)}, u32[]{:S(2)}, u32[]{:S(2)}) async-start(bf16[8,128,1024]{1,2,0:T(8,128)(2,1)} %broadcast_in_dim.38), calls=%async_computation | async-start | bytes 4194304 | tf_op jit(solution)/shard_map/all_to_all | solution.py:19
  15.6 11.6 %copy-start.4 = (s32[4,2048]{1,0:T(4,128)S(1)}, s32[4,2048]{1,0:T(4,128)}, u32[]{:S(2)}) copy-start(s32[4,2048]{1,0:T(4,128)} %param.19) | copy-start | bytes 98308
  53.7 9.0 %copy-start.2 = (bf16[4,2048,64]{1,2,0:T(8,128)(2,1)S(1)}, bf16[4,2048,64]{1,2,0:T(8,128)(2,1)}, u32[]{:S(2)}) copy-start(bf16[4,2048,64]{1,2,0:T(8,128)(2,1)} %param.17) | copy-start | bytes 3145732
  53.7 9.0 %copy-start.3 = (f32[4,2048]{1,0:T(4,128)S(1)}, f32[4,2048]{1,0:T(4,128)}, u32[]{:S(2)}) copy-start(f32[4,2048]{1,0:T(4,128)} %param.18) | copy-start | bytes 98308
  53.7 9.0 %copy-start.10 = (f32[64]{0:T(128)S(1)}, f32[64]{0:T(128)}, u32[]{:S(2)}) copy-start(f32[64]{0:T(128)} %param.20) | copy-start | bytes 772
  63.4 73.6 %copy-start.11 = (bf16[64,256]{1,0:T(8,128)(2,1)S(1)}, bf16[64,256]{1,0:T(8,128)(2,1)}, u32[]{:S(2)}) copy-start(bf16[64,256]{1,0:T(8,128)(2,1)} %param.22) | copy-start | bytes 98308
  63.5 73.6 %copy-start.12 = (f32[256]{0:T(256)S(1)}, f32[256]{0:T(256)}, u32[]{:S(2)}) copy-start(f32[256]{0:T(256)} %param.23) | copy-start | bytes 3076
  63.5 73.6 %copy-start.13 = (f32[64]{0:T(128)S(1)}, f32[64]{0:T(128)}, u32[]{:S(2)}) copy-start(f32[64]{0:T(128)} %param.21) | copy-start | bytes 772
  63.5 73.8 %copy-start.5 = (bf16[256,64]{0,1:T(8,128)(2,1)S(1)}, bf16[256,64]{0,1:T(8,128)(2,1)}, u32[]{:S(2)}) copy-start(bf16[256,64]{0,1:T(8,128)(2,1)} %param.26) | copy-start | bytes 98308
  63.5 73.8 %copy-start.8 = (f32[256]{0:T(256)S(1)}, f32[256]{0:T(256)}, u32[]{:S(2)}) copy-start(f32[256]{0:T(256)} %param.25) | copy-start | bytes 3076
  63.5 73.8 %copy-start.9 = (f32[64]{0:T(128)S(1)}, f32[64]{0:T(128)}, u32[]{:S(2)}) copy-start(f32[64]{0:T(128)} %param.27) | copy-start | bytes 772
  127.4 8.7 %all-to-all-start.2 = ((f32[8,1,1024]{2,1,0:T(1,128)}), f32[8,1,1024]{2,1,0:T(1,128)S(1)}, u32[]{:S(2)}, u32[]{:S(2)}) async-start(f32[8,1,1024]{2,1,0:T(1,128)} %reshape.106), calls=%async_computation.2 | async-start | bytes 65536 | tf_op jit(solution)/shard_map/all_to_all | solution.py:19
  137.6 35.9 %copy-start.6 = (bf16[16,64]{1,0:T(8,128)(2,1)}, bf16[16,64]{1,0:T(8,128)(2,1)S(1)}, u32[]{:S(2)}) copy-start(bf16[16,64]{1,0:T(8,128)(2,1)S(1)} %fusion.11) | copy-start | bytes 6148
  138.3 11.0 %all-to-all-start.3 = ((bf16[16,2,512]{2,1,0:T(2,128)(2,1)}), bf16[16,2,512]{2,1,0:T(2,128)(2,1)S(1)}, u32[]{:S(2)}, u32[]{:S(2)}) async-start(bf16[16,2,512]{2,1,0:T(2,128)(2,1)} %reshape.108), calls=%async_computation.3 | async-start | bytes 65536 | tf_op jit(solution)/shard_map/all_to_all | solution.py:19
  141.8 116.5 %reduce-scatter.2.cloned.1.call-start = ((), (), s32[]{:S(2)}) async-start(), calls=%async_computation.6 | async-start | bytes 4718592 | tf_op jit(solution)/shard_map/reduce_scatter | solution.py:119
  221.1 55.6 %copy-start.1 = (bf16[256,256]{1,0:T(8,128)(2,1)S(1)}, bf16[256,256]{1,0:T(8,128)(2,1)}, u32[]{:S(2)}) copy-start(bf16[256,256]{1,0:T(8,128)(2,1)} %param.24) | copy-start | bytes 393220
Sparse Core Ops, SparseCore 0:
  224.2 33.9 reduce-scatter.1
where the time goes:
time: 285 us; the launch traced here: 284 us
  local copies, waits for them, and re-layouts  78.5 us (28%)
  other arithmetic  63.5 us (22%)
  waiting for transfers between devices  62 us (22%)
  blocking collectives  31.1 us (11%)
  matrix products  21.7 us (8%)
  between operations  14.4 us (5%)
  starting transfers between devices  12.4 us (4%)
    scatter-add x1, other arithmetic, shards(): jax.ops.segment_sum(weighted_feat.reshape(-1, feat_width), centre_ids.res...  44.3 us
    reduce_scatter x1, waiting for transfers between devices, shards(): lax.psum_scatter(whole.reshape(basis_count, basis_count), 'mat', scatter_...  34.2 us
    all_to_all x2, blocking collectives, summed_on_arrival(): parts = lax.all_to_all(cut_along(value, dim, peers), axis, 0, 0, tiled=True)  31.1 us
    all_to_all x3, waiting for transfers between devices, sent_to_all(): return lax.all_to_all(copies, axis, split_axis=0, concat_axis=0, tiled=True)  27.9 us
    gather x1, local copies, waits for them, and re-layouts, shards(): nearest = everyone[centre_ids].astype(jnp.float32)  24 us
    unnamed x41, local copies, waits for them, and re-layouts  17.6 us
    scatter-add x1, other arithmetic, shards(): whole.at[tile_ids[:, :, None], :, tile_ids[:, None, :]].add(tile_blocks)  14 us
    dot_general x1, matrix products, shards(): jnp.einsum('bpa,bpc->bac', basis_values, weighted, preferred_element_type...  12.2 us
  transfers between devices with their start and end apart: 4, of which 4 were waited for; matrix products, arithmetic and copies ran while one was open for 4% of the time, Pallas kernels for 0%

commit v1 on v0

v1 whole, which is shorter than its diff:
```python
import functools
import math

import jax
import jax.numpy as jnp
from jax import lax
from jax.experimental import pallas as pl
from jax.experimental.pallas import tpu as pltpu
from jax.sharding import PartitionSpec as P

BF = jnp.bfloat16
F32 = jnp.float32
LANES = (((1,), (1,)), ((), ()))
MB = 1 << 20
CENT_DEV = 16


def whole(shape):
    return pl.BlockSpec(shape, lambda *_: (0,) * len(shape))


def in_hbm(x):
    return pltpu.with_memory_space_constraint(x, pltpu.HBM)


def silu(v):
    return v / (1.0 + jnp.exp(-v))


def one_hot(ids_row, centres):
    rows = lax.broadcasted_iota(jnp.int32, (centres, ids_row.shape[1]), 0)
    return (rows == ids_row).astype(F32).astype(BF)


def transpose_kernel(x_ref, o_ref):
    o_ref[0] = x_ref[0].T


def transposed(x, chunk):
    batches, points, orbitals = x.shape
    return pl.pallas_call(
        transpose_kernel,
        grid=(batches, points // chunk),
        in_specs=[pl.BlockSpec((1, chunk, orbitals), lambda b, r: (b, r, 0))],
        out_specs=pl.BlockSpec((1, orbitals, chunk), lambda b, r: (b, 0, r)),
        out_shape=jax.ShapeDtypeStruct((batches, orbitals, points), x.dtype),
        compiler_params=pltpu.CompilerParams(vmem_limit_bytes=16 * MB),
        cost_estimate=pl.CostEstimate(
            flops=0, bytes_accessed=4 * x.size, transcendentals=0
        ),
    )(in_hbm(x))


def sum_kernel(x_ref, o_ref):
    total = jnp.sum(x_ref[...].astype(F32), axis=0).astype(o_ref.dtype)
    o_ref[...] = jnp.broadcast_to(total, o_ref.shape)


def summed(x, copies=()):
    return pl.pallas_call(
        sum_kernel,
        out_shape=jax.ShapeDtypeStruct((*copies, *x.shape[1:]), x.dtype),
        compiler_params=pltpu.CompilerParams(vmem_limit_bytes=8 * MB),
    )(x)


def slab_copies(pos_ref, chips, slabs, table_ref, sem_ref):
    core, z = pos_ref[0], pos_ref[2]
    half = table_ref.shape[1] // 2
    top, bottom = pl.ds(0, half), pl.ds(half, half)
    every = pl.ds(0, 2 * half)
    places = [(0, every), (chips - 1, every), (1, every), (2, top), (2, bottom)]
    copies = []
    for side in range(2):
        for k, (shift, rows) in enumerate(places):
            chip = lax.rem(z + shift, chips)
            slot = 2 * chip + (core if side == 0 else 1 - core)
            n = side * len(places) + k
            copies.append(
                pltpu.make_async_copy(slabs[n], table_ref.at[slot, rows], sem_ref.at[n])
            )
    return copies


def density_kernel(
    tile, chunk, chips, tid_ref, pos_ref, *refs
):
    slabs, refs = refs[:10], refs[10:]
    density_body(tile, chunk, chips, tid_ref, pos_ref, slabs, *refs)


def density_body(
    tile, chunk, chips, tid_ref, pos_ref, slabs, xt_ref, desc_ref, w_ref, ids_ref, scale_ref,
    dens_ref, sum_ref, table_ref, panel_ref, acc_ref, sem_ref,
):
    b, part = pl.program_id(0), pl.program_id(1)
    parts = pl.num_programs(1)
    orbitals, points = xt_ref.shape[1:]
    per_batch = orbitals // tile
    feats = desc_ref.shape[1]
    centres = sum_ref.shape[2]

    @pl.when((b == 0) & (part == 0))
    def _():
        copies = slab_copies(pos_ref, chips, slabs, table_ref, sem_ref)
        for copy in copies:
            copy.start()
        for copy in copies:
            copy.wait()

    @pl.when(part == 0)
    def _():
        for i in range(per_batch):
            ti = tid_ref[b, i]
            for j in range(per_batch):
                tj = tid_ref[b, j]
                panel_ref[i * tile : (i + 1) * tile, j * tile : (j + 1) * tile] = table_ref[
                    ti, :, pl.ds(pl.multiple_of(tj * tile, tile), tile)
                ]

    gathered = jnp.zeros(acc_ref.shape[1:], F32)
    for r in range(points // chunk):
        at = slice(r * chunk, (r + 1) * chunk)
        out = pl.ds(pl.multiple_of(part * points + r * chunk, chunk), chunk)
        xt = xt_ref[0, :, at]
        q = jnp.dot(panel_ref[...], xt, preferred_element_type=F32)
        dens = jnp.sum(xt.astype(F32) * q, axis=0, keepdims=True)
        dens_ref[pl.ds(b, 1), out] = dens
        f = silu(dens * scale_ref[...] + desc_ref[0, :, at].astype(F32))
        f = f * w_ref[pl.ds(b, 1), out]
        high = f.astype(BF)
        low = (f - high.astype(F32)).astype(BF)
        both = jnp.concatenate([high, low], axis=0)
        hot = one_hot(ids_ref[pl.ds(b, 1), out], centres)
        gathered += lax.dot_general(both, hot, LANES, preferred_element_type=F32)
    acc_ref[b * parts + part] = gathered

    @pl.when((b == pl.num_programs(0) - 1) & (part == parts - 1))
    def _():
        total = jnp.sum(acc_ref[...], axis=0)
        total = (total[:feats] + total[feats:]).astype(sum_ref.dtype)
        sum_ref[...] = jnp.broadcast_to(total, sum_ref.shape)


def potential_kernel(
    tile, chunk, factor, tid_ref, pos_ref, sums_ref, gain_ref, w1_ref, b1_ref, w2_ref, b2_ref, w3_ref,
    b3_ref, dens_ref, desc_ref, w_ref, ids_ref, xt_ref, x_ref, own_ref, other_ref, cf_ref,
    cft_ref, cfall_ref, wt_ref, acc_ref,
):
    b = pl.program_id(0)
    orbitals, points = xt_ref.shape[1:]
    per_batch = orbitals // tile
    centres = cft_ref.shape[1]
    mine = cf_ref.shape[0]

    @pl.when(b == 0)
    def _():
        acc_ref[...] = jnp.zeros_like(acc_ref)
        total = jnp.sum(sums_ref[...].astype(F32), axis=0)
        inverse = lax.rsqrt(jnp.mean(total * total, axis=0, keepdims=True) + 1e-05)
        normed = ((total * inverse).T * gain_ref[...]).astype(BF)
        one = silu(
            jnp.dot(normed, w1_ref[...], preferred_element_type=F32) + b1_ref[...]
        ).astype(BF)
        two = silu(
            jnp.dot(one, w2_ref[...], preferred_element_type=F32) + b2_ref[...]
        ).astype(BF)
        feats = lax.dot_general(two, w3_ref[...], LANES, preferred_element_type=F32) + b3_ref[...]
        cfall_ref[...] = feats
        cf_ref[...] = cfall_ref[pl.ds(pl.multiple_of(pos_ref[1] * mine, 8), mine), :].astype(BF)
        cft_ref[...] = feats.T.astype(BF)

    for r in range(points // chunk):
        at = slice(r * chunk, (r + 1) * chunk)
        hot = one_hot(ids_ref[pl.ds(b, 1), at], centres)
        nearest = jnp.dot(cft_ref[...], hot, preferred_element_type=F32)
        inner = jnp.sum(nearest * desc_ref[0, :, at].astype(F32), axis=0, keepdims=True)
        v = w_ref[pl.ds(b, 1), at] * dens_ref[pl.ds(b, 1), at] * inner * factor
        wt_ref[:, at] = (v * xt_ref[0, :, at].astype(F32)).astype(BF)
    for i in range(per_batch):
        rows = slice(i * tile, (i + 1) * tile)
        block = jnp.dot(wt_ref[rows, :], x_ref[0], preferred_element_type=F32)
        for j in range(per_batch):
            acc_ref[tid_ref[b, i], tid_ref[b, j]] += block[:, j * tile : (j + 1) * tile]

    @pl.when(b == pl.num_programs(0) - 1)
    def _():
        core = pos_ref[0]
        for z in range(own_ref.shape[0]):
            for i in range(own_ref.shape[1]):
                own_ref[z, i] = acc_ref[i, 2 * z + core]
                other_ref[z, i] = acc_ref[i, 2 * z + 1 - core].astype(BF)


def shards(
    basis_values, tile_ids, density_matrix, descriptors, grid_weights, centre_ids, density_scale,
    norm_gain, w_first, b_first, w_second, b_second, w_third, b_third,
):
    batches, points, orbitals = basis_values.shape
    per_batch = tile_ids.shape[1]
    tile = orbitals // per_batch
    basis = density_matrix.shape[1]
    tiles = basis // tile
    feats = descriptors.shape[2]
    mats = lax.axis_size("mat")
    columns = lax.axis_size("pts")
    chips = mats // 2
    mine = CENT_DEV
    centres = mine * columns
    chunk = 512
    parts = 1
    here, there = lax.axis_index("mat"), lax.axis_index("pts")
    pos = jnp.stack([here % 2, there, here // 2]).astype(jnp.int32)
    swap = [(i, i ^ 1) for i in range(mats)]
    up = [(i, (i + 2) % mats) for i in range(mats)]
    down = [(i, (i - 2) % mats) for i in range(mats)]
    across = [(i, (i + 4) % mats) for i in range(mats)]
    same_core = [
        [m * columns + p for m in range(c, mats, 2) for p in range(columns)] for c in range(2)
    ]
    desc = jnp.swapaxes(descriptors, 1, 2)
    scale = density_scale.reshape(feats, 1)

    top = lax.ppermute(density_matrix[: tile // 2], "mat", across)
    bottom = lax.ppermute(density_matrix[tile // 2 :], "mat", across)
    below = lax.ppermute(density_matrix, "mat", up)
    above = lax.ppermute(density_matrix, "mat", down)
    xt = transposed(basis_values, points)
    top, bottom, below, above, xt = lax.optimization_barrier((top, bottom, below, above, xt))
    slabs = [density_matrix, below, above, top, bottom]
    slabs += [lax.ppermute(slab, "mat", swap) for slab in slabs]

    density, partial = pl.pallas_call(
        functools.partial(density_kernel, tile, chunk, chips),
        grid_spec=pltpu.PrefetchScalarGridSpec(
            num_scalar_prefetch=2,
            grid=(batches, parts),
            in_specs=[
                *[pl.BlockSpec(memory_space=pl.ANY)] * len(slabs),
                pl.BlockSpec((1, orbitals, points // parts), lambda b, r, *_: (b, 0, r)),
                pl.BlockSpec((1, feats, points // parts), lambda b, r, *_: (b, 0, r)),
                whole((batches, points)),
                whole((batches, points)),
                whole((feats, 1)),
            ],
            out_specs=[whole((batches, points)), whole((mats, feats, centres))],
            scratch_shapes=[
                pltpu.VMEM((tiles, tile, basis), BF),
                pltpu.VMEM((orbitals, orbitals), BF),
                pltpu.VMEM((batches * parts, 2 * feats, centres), F32),
                pltpu.SemaphoreType.DMA((len(slabs),)),
            ],
        ),
        out_shape=[
            jax.ShapeDtypeStruct((batches, points), F32),
            jax.ShapeDtypeStruct((mats, feats, centres), BF),
        ],
        compiler_params=pltpu.CompilerParams(vmem_limit_bytes=16 * MB),
        cost_estimate=pl.CostEstimate(
            flops=2 * batches * points * orbitals * orbitals,
            bytes_accessed=2 * basis_values.size,
            transcendentals=descriptors.size,
        ),
    )(tile_ids, pos, *slabs, in_hbm(xt), desc, grid_weights, centre_ids, scale)

    first = summed(lax.all_to_all(partial, "mat", 0, 0, tiled=True), (columns,))
    sums = lax.all_to_all(first, "pts", 0, 0, tiled=True)

    all_batches = batches * mats * columns
    factor = tiles / (per_batch * math.sqrt(points * feats * all_batches))
    hidden = w_first.shape[1]
    own, other, centre_features = pl.pallas_call(
        functools.partial(potential_kernel, tile, chunk, factor),
        grid_spec=pltpu.PrefetchScalarGridSpec(
            num_scalar_prefetch=2,
            grid=(batches,),
            in_specs=[
                whole((columns, feats, centres)),
                whole((1, feats)),
                whole((feats, hidden)),
                whole((1, hidden)),
                whole((hidden, hidden)),
                whole((1, hidden)),
                whole((feats, hidden)),
                whole((1, feats)),
                whole((batches, points)),
                pl.BlockSpec((1, feats, points), lambda b, *_: (b, 0, 0)),
                whole((batches, points)),
                whole((batches, points)),
                pl.BlockSpec((1, orbitals, points), lambda b, *_: (b, 0, 0)),
                pl.BlockSpec((1, points, orbitals), lambda b, *_: (b, 0, 0)),
            ],
            out_specs=[
                whole((chips, tiles, tile, tile)),
                whole((chips, tiles, tile, tile)),
                whole((mine, feats)),
            ],
            scratch_shapes=[
                pltpu.VMEM((feats, centres), BF),
                pltpu.VMEM((centres, feats), F32),
                pltpu.VMEM((orbitals, points), BF),
                pltpu.VMEM((tiles, tiles, tile, tile), F32),
            ],
        ),
        out_shape=[
            jax.ShapeDtypeStruct((chips, tiles, tile, tile), F32),
            jax.ShapeDtypeStruct((chips, tiles, tile, tile), BF),
            jax.ShapeDtypeStruct((mine, feats), BF),
        ],
        compiler_params=pltpu.CompilerParams(vmem_limit_bytes=28 * MB),
        cost_estimate=pl.CostEstimate(
            flops=2 * batches * points * orbitals * orbitals,
            bytes_accessed=4 * basis_values.size,
            transcendentals=2 * centres * hidden,
        ),
    )(
        tile_ids, pos, sums, norm_gain.reshape(1, feats), w_first, b_first.reshape(1, hidden),
        w_second, b_second.reshape(1, hidden), w_third.T, b_third.reshape(1, feats), density, desc,
        grid_weights, centre_ids, xt, basis_values,
    )

    joined = (own + lax.ppermute(other, "mat", swap).astype(F32)).astype(BF)
    joined = joined.reshape(chips * columns, basis // columns, tile)
    pieces = lax.all_to_all(
        joined, ("mat", "pts"), 0, 0, tiled=True, axis_index_groups=same_core
    )
    return (summed(pieces).T, centre_features)


def solution(mesh):
    return jax.shard_map(
        shards,
        mesh=mesh,
        in_specs=(
            P(("mat", "pts"), None, None),
            P(("mat", "pts"), None),
            P("mat", None),
            P(("mat", "pts"), None, None),
            P(("mat", "pts"), None),
            P(("mat", "pts"), None),
            P(), P(), P(), P(), P(), P(), P(), P(),
        ),
        out_specs=(P("mat", "pts"), P("pts", None)),
        check_vma=False,
    )
```

time: 285 us -> 96.9 us (0.34)
  local copies, waits for them, and re-layouts: 78.5 us -> 4.43 us
  other arithmetic: 63.5 us -> 0.4 us
  waiting for transfers between devices: 62 us -> 3.81 us
  Pallas kernels: 0 us -> 25.6 us
  matrix products: 21.7 us -> 0 us
  blocking collectives: 31.1 us -> 52.4 us
  between operations: 14.4 us -> 0.9 us
  starting transfers between devices: 12.4 us -> 9.16 us
    scatter-add x2 -> x0, other arithmetic: 58.4 us -> none  [the longest x1 44.3 us: shards(): jax.ops.segment_sum(weighted_feat.reshape(-1, feat_width), centre_ids.res...]
    reduce_scatter x1 -> x0, waiting for transfers between devices: 34.2 us -> none  [shards(): lax.psum_scatter(whole.reshape(basis_count, basis_count), 'mat', scatter_...]
    all_to_all x3 -> x0, waiting for transfers between devices: 27.9 us -> none  [sent_to_all(): return lax.all_to_all(copies, axis, split_axis=0, concat_axis=0, tiled=True)]
    gather x2 -> x0, local copies, waits for them, and re-layouts: 26.6 us -> none  [the longest x1 24 us: shards(): nearest = everyone[centre_ids].astype(jnp.float32)]
    pallas_call x0 -> x5, Pallas kernels: none -> 25.6 us  [the longest x1 11.2 us: shards(): pl.pallas_call(functools.partial(density_kernel, tile, chunk, chips), gri...]
    dot_general x4 -> x0, matrix products: 21.7 us -> none  [the longest x1 12.2 us: shards(): jnp.einsum('bpa,bpc->bac', basis_values, weighted, preferred_element_type...]
    all_to_all x2 -> x3, blocking collectives: 31.1 us -> 52.4 us  [the longest x1 23.7 us: shards(): lax.all_to_all(joined, ('mat', 'pts'), 0, 0, tiled=True, axis_index_group...]
    unnamed x41 -> x34, local copies, waits for them, and re-layouts: 17.6 us -> 3.35 us
  transfers between devices with their start and end apart: 4 -> 10, of which waited for: 4 -> 3; matrix products, arithmetic and copies ran while one was open for 4% -> 1% of each run, Pallas kernels for 0% -> 5%
where the time goes in v1:
time: 96.9 us; the launch traced here: 96.6 us
  blocking collectives  52.4 us (54%)
  Pallas kernels  25.6 us (26%)
  starting transfers between devices  9.16 us (9%)
  local copies, waits for them, and re-layouts  4.43 us (5%)
  waiting for transfers between devices  3.81 us (4%)
    all_to_all x1, blocking collectives, shards(): lax.all_to_all(joined, ('mat', 'pts'), 0, 0, tiled=True, axis_index_group...  23.7 us
    all_to_all x1, blocking collectives, shards(): sums = lax.all_to_all(first, 'pts', 0, 0, tiled=True)  18 us
    pallas_call x1, Pallas kernels, shards(): pl.pallas_call(functools.partial(density_kernel, tile, chunk, chips), gri...  11.2 us
    all_to_all x1, blocking collectives, shards(): first = summed(lax.all_to_all(partial, 'mat', 0, 0, tiled=True), (columns,))  10.7 us
    pallas_call x1, Pallas kernels, shards(): pl.pallas_call(functools.partial(potential_kernel, tile, chunk, factor),...  8.28 us
    pallas_call x1, Pallas kernels, transposed(): pl.pallas_call(transpose_kernel, grid=(batches, points // chunk), in_spec...  5.29 us
    unnamed x34, local copies, waits for them, and re-layouts  3.35 us
    ppermute x1, waiting for transfers between devices, shards(): joined = (own + lax.ppermute(other, 'mat', swap).astype(F32)).astype(BF)  2.66 us
  transfers between devices with their start and end apart: 10, of which 3 were waited for; matrix products, arithmetic and copies ran while one was open for 1% of the time, Pallas kernels for 5%

profile of v1, /device:TPU:0, one launch (start us, length us, event | category | flops | bytes accessed | tf_op | source)
XLA Modules:
  0.0 96.6 jit_solution(15182568685171507289)
XLA Ops:
  0.6 2.1 %collective-permute-start.2 = (bf16[128,1024]{1,0:T(8,128)(2,1)}, bf16[128,1024]{1,0:T(8,128)(2,1)S(1)}, u32[]{:S(2)}, u32[]{:S(2)}) collective-permute-start(bf16[128,1024]{1,0:T(8,128)(2,1)} %refs_0_.1), channel_id=1, source_target_pairs={{0,32},{16,48},{32,64},{48,80},{64,96},{80,112},{96,0},{112,16},{1... | collective-permute-start | bytes 786440 | tf_op jit(solution)/shard_map/ppermute | solution.py:226
  2.7 2.2 %collective-permute-start.3 = (bf16[128,1024]{1,0:T(8,128)(2,1)}, bf16[128,1024]{1,0:T(8,128)(2,1)S(1)}, u32[]{:S(2)}, u32[]{:S(2)}) collective-permute-start(bf16[128,1024]{1,0:T(8,128)(2,1)} %refs_0_.1), channel_id=1, source_target_pairs={{0,96},{16,112},{32,0},{48,16},{64,32},{80,48},{96,64},{112,80},{1... | collective-permute-start | bytes 786440 | tf_op jit(solution)/shard_map/ppermute | solution.py:227
  4.9 1.0 %fusion = (bf16[64,1024]{1,0:T(8,128)(2,1)S(1)}, bf16[64,1024]{1,0:T(8,128)(2,1)S(1)}) fusion(bf16[128,1024]{1,0:T(8,128)(2,1)} %refs_0_.1), kind=kLoop, calls=%fused_computation.2 | loop fusion | bytes 524288 | tf_op jit(solution)/shard_map/slice | solution.py:225
  5.9 1.9 %collective-permute-start.1 = (bf16[64,1024]{1,0:T(8,128)(2,1)S(1)}, bf16[64,1024]{1,0:T(8,128)(2,1)S(1)}, u32[]{:S(2)}, u32[]{:S(2)}) collective-permute-start(bf16[64,1024]{1,0:T(8,128)(2,1)S(1)} %get-tuple-element.22), channel_id=1, source_target_pairs={{0,64},{16,80},{32,96},{48,112},{64,0},{80,16},{96,32},{112,48},{1... | collective-permute-start | bytes 393224 | tf_op jit(solution)/shard_map/ppermute | solution.py:225
  7.8 0.0 copy-start.2
  7.8 0.0 copy-start.3
  7.8 0.0 copy-start.5
  7.8 0.0 copy-start.6
  7.8 0.0 copy-start.9
  7.8 1.8 %collective-permute-start = (bf16[64,1024]{1,0:T(8,128)(2,1)S(1)}, bf16[64,1024]{1,0:T(8,128)(2,1)S(1)}, u32[]{:S(2)}, u32[]{:S(2)}) collective-permute-start(bf16[64,1024]{1,0:T(8,128)(2,1)S(1)} %get-tuple-element.23), channel_id=1, source_target_pairs={{0,64},{16,80},{32,96},{48,112},{64,0},{80,16},{96,32},{112,48},{1... | collective-permute-start | bytes 393224 | tf_op jit(solution)/shard_map/ppermute | solution.py:224
  9.6 0.0 collective-permute-start.4
  9.6 5.3 %shard_map.149.refs_10_.xt_ref = bf16[4,512,2048]{2,1,0:T(8,128)(2,1)S(1)} custom-call(bf16[4,2048,512]{2,1,0:T(8,128)(2,1)} %x_ref.3), custom_call_target="tpu_custom_call" | custom-call | bytes 16777216 | tf_op jit(solution)/shard_map/pallas_call | solution.py:41
  14.9 0.0 copy-start
  14.9 3.3 %copy-done = bf16[4,512,2048]{2,1,0:T(8,128)(2,1)} copy-done((bf16[4,512,2048]{2,1,0:T(8,128)(2,1)}, bf16[4,512,2048]{2,1,0:T(8,128)(2,1)S(1)}, u32[]{:S(2)}) %copy-start) | copy-done | bytes 8388632
  18.2 0.0 collective-permute-done.1.refs_4_
  18.2 0.0 collective-permute-done.refs_3_
  18.2 0.0 collective-permute-done.2.refs_1_
  18.2 0.0 collective-permute-done.3.refs_2_
  18.2 0.6 collective-permute-start.5
  18.8 0.1 collective-permute-start.6
  18.9 0.4 collective-permute-start.7
  19.3 0.1 collective-permute-start.8
  19.4 0.0 copy-done.14
  19.4 0.1 copy.16.refs_14_
  19.5 0.1 pad_add_fusion.pos_ref
  19.6 0.0 collective-permute-done.4.refs_5_
  19.6 0.9 collective-permute-done.7.refs_8_
  20.5 0.2 collective-permute-done.8.refs_9_
  20.7 0.0 collective-permute-done.5.refs_6_
  20.7 0.0 collective-permute-done.6.refs_7_
  20.7 0.0 copy-done.2
  20.7 0.0 copy-done.3
  20.8 0.0 copy-done.5
  20.8 0.0 copy-done.6
  20.8 0.0 copy-done.9
  20.8 0.0 slice-start.1
  20.8 0.0 copy-start.1
  20.8 11.2 %shard_map.150 = (f32[4,2048]{1,0:T(4,128)S(1)}, bf16[8,64,256]{2,1,0:T(8,128)(2,1)S(1)}) custom-call(s32[4,4]{1,0:T(4,128)S(1)} %copy-done.9, s32[3]{0:T(128)S(1)} %pad_add_fusion.pos_ref, bf16[128,1024]{1,0:T(8,128)(2,1)S(1)} %copy-done.3, bf16[128,1024]{1,0:T(8,128)(2,1)S(1)} %collective-permute-done.2.refs_1_, ...), custom_call_target="tpu_custom_call" | custom-call | flops 4294967296 | bytes 8388608 | tf_op jit(solution)/shard_map/pallas_call | solution.py:233
  32.0 0.0 copy-start.4
  32.0 0.0 copy-start.7
  32.0 0.0 copy-start.8
  32.0 0.0 copy-start.10
  32.1 0.0 copy-start.11
  32.1 0.0 copy-start.12
  32.1 0.0 copy-start.13
  32.1 10.7 %all_to_all.15.x_ref = bf16[8,64,256]{2,1,0:T(8,128)(2,1)S(1)} all-to-all(bf16[8,64,256]{2,1,0:T(8,128)(2,1)S(1)} %get-tuple-element.17), channel_id=1, replica_groups=mesh['mat'=8,'pts'=16] {'mat'}, dimensions={0} | all-to-all | bytes 524288 | tf_op jit(solution)/shard_map/all_to_all | solution.py:266
  42.8 0.1 shard_map.151
  42.8 18.0 %all_to_all.16.sums_ref = bf16[16,64,256]{2,1,0:T(8,128)(2,1)S(1)} all-to-all(bf16[16,64,256]{2,1,0:T(8,128)(2,1)S(1)} %shard_map.151), channel_id=1, replica_groups=mesh['mat'=8,'pts'=16] {'pts'}, dimensions={0} | all-to-all | bytes 1048576 | tf_op jit(solution)/shard_map/all_to_all | solution.py:267
  60.8 0.0 slice-done
  60.9 0.0 slice-done.1
  60.9 0.0 copy-done.1
  60.9 0.0 copy-done.4
  60.9 0.0 copy-done.7
  60.9 0.0 copy-done.8
  60.9 0.0 copy-done.10
  60.9 0.0 copy-done.11
  60.9 0.0 copy-done.12
  60.9 0.0 copy-done.13
  60.9 8.3 %shard_map.152 = (f32[4,8,128,128]{3,2,1,0:T(8,128)S(1)}, bf16[4,8,128,128]{3,2,1,0:T(8,128)(2,1)S(1)}, bf16[16,64]{1,0:T(8,128)(2,1)}) custom-call(s32[4,4]{1,0:T(4,128)S(1)} %copy-done.9, s32[3]{0:T(128)S(1)} %pad_add_fusion.pos_ref, bf16[16,64,256]{2,1,0:T(8,128)(2,1)S(1)} %all_to_all.16.sums_ref, f32[1,64]{1,0:T(1,128)S(1)} %bitcast.19, ...), custom_call_target="tpu_custom_call" | custom-call | flops 4294967296 | bytes 16777216 | tf_op jit(solution)/shard_map/pallas_call | solution.py:272
  69.2 0.0 collective-permute-start.9
  69.2 2.7 %collective-permute-done.9 = bf16[4,8,128,128]{3,2,1,0:T(8,128)(2,1)S(1)} collective-permute-done((bf16[4,8,128,128]{3,2,1,0:T(8,128)(2,1)S(1)}, bf16[4,8,128,128]{3,2,1,0:T(8,128)(2,1)S(1)}, u32[]{:S(2)}, u32[]{:S(2)}) %collective-permute-start.9) | collective-permute-done | bytes 1048608 | tf_op jit(solution)/shard_map/ppermute | solution.py:322
  71.9 0.3 add_convert_fusion
  72.2 23.7 %all_to_all.17.x_ref = bf16[64,64,128]{2,1,0:T(8,128)(2,1)S(1)} all-to-all(bf16[64,64,128]{2,1,0:T(8,128)(2,1)S(1)} %bitcast.21), channel_id=1, replica_groups={{0,1,2,3,4,5,6,7,8,9,10,11,12,13,14,15,32,33,34,35,36,37,38,39,40,41,42..., dimensions={0} | all-to-all | bytes 2097152 | tf_op jit(solution)/shard_map/all_to_all | solution.py:324
  95.9 0.8 shard_map.153
  (3 shorter events, 0.0 us)
Async XLA Ops:
  0.6 17.6 %collective-permute-start.2 = (bf16[128,1024]{1,0:T(8,128)(2,1)}, bf16[128,1024]{1,0:T(8,128)(2,1)S(1)}, u32[]{:S(2)}, u32[]{:S(2)}) collective-permute-start(bf16[128,1024]{1,0:T(8,128)(2,1)} %refs_0_.1), channel_id=1, source_target_pairs={{0,32},{16,48},{32,64},{48,80},{64,96},{80,112},{96,0},{112,16},{1... | collective-permute-start | bytes 786440 | tf_op jit(solution)/shard_map/ppermute | solution.py:226
  2.7 15.5 %collective-permute-start.3 = (bf16[128,1024]{1,0:T(8,128)(2,1)}, bf16[128,1024]{1,0:T(8,128)(2,1)S(1)}, u32[]{:S(2)}, u32[]{:S(2)}) collective-permute-start(bf16[128,1024]{1,0:T(8,128)(2,1)} %refs_0_.1), channel_id=1, source_target_pairs={{0,96},{16,112},{32,0},{48,16},{64,32},{80,48},{96,64},{112,80},{1... | collective-permute-start | bytes 786440 | tf_op jit(solution)/shard_map/ppermute | solution.py:227
  5.9 12.3 %collective-permute-start.1 = (bf16[64,1024]{1,0:T(8,128)(2,1)S(1)}, bf16[64,1024]{1,0:T(8,128)(2,1)S(1)}, u32[]{:S(2)}, u32[]{:S(2)}) collective-permute-start(bf16[64,1024]{1,0:T(8,128)(2,1)S(1)} %get-tuple-element.22), channel_id=1, source_target_pairs={{0,64},{16,80},{32,96},{48,112},{64,0},{80,16},{96,32},{112,48},{1... | collective-permute-start | bytes 393224 | tf_op jit(solution)/shard_map/ppermute | solution.py:225
  7.8 11.7 %copy-start.14 = (f32[64]{0:T(128)S(1)}, f32[64]{0:T(128)}, u32[]{:S(2)}) copy-start(f32[64]{0:T(128)} %param.20) | copy-start | bytes 772
  7.8 13.0 %copy-start.2 = (bf16[4,2048,64]{1,2,0:T(8,128)(2,1)S(1)}, bf16[4,2048,64]{1,2,0:T(8,128)(2,1)}, u32[]{:S(2)}) copy-start(bf16[4,2048,64]{1,2,0:T(8,128)(2,1)} %param.17) | copy-start | bytes 3145732
  7.8 13.0 %copy-start.3 = (bf16[128,1024]{1,0:T(8,128)(2,1)S(1)}, bf16[128,1024]{1,0:T(8,128)(2,1)}, u32[]{:S(2)}) copy-start(bf16[128,1024]{1,0:T(8,128)(2,1)} %refs_0_.1) | copy-start | bytes 786436
  7.8 13.0 %copy-start.5 = (f32[4,2048]{1,0:T(4,128)S(1)}, f32[4,2048]{1,0:T(4,128)}, u32[]{:S(2)}) copy-start(f32[4,2048]{1,0:T(4,128)} %w_ref.1) | copy-start | bytes 98308
  7.8 13.0 %copy-start.6 = (s32[4,2048]{1,0:T(4,128)S(1)}, s32[4,2048]{1,0:T(4,128)}, u32[]{:S(2)}) copy-start(s32[4,2048]{1,0:T(4,128)} %ids_ref.1) | copy-start | bytes 98308
  7.8 13.0 %copy-start.9 = (s32[4,4]{1,0:T(4,128)S(1)}, s32[4,4]{1,0:T(4,128)}, u32[]{:S(2)}) copy-start(s32[4,4]{1,0:T(4,128)} %tid_ref.3) | copy-start | bytes 196
  7.8 10.4 %collective-permute-start = (bf16[64,1024]{1,0:T(8,128)(2,1)S(1)}, bf16[64,1024]{1,0:T(8,128)(2,1)S(1)}, u32[]{:S(2)}, u32[]{:S(2)}) collective-permute-start(bf16[64,1024]{1,0:T(8,128)(2,1)S(1)} %get-tuple-element.23), channel_id=1, source_target_pairs={{0,64},{16,80},{32,96},{48,112},{64,0},{80,16},{96,32},{112,48},{1... | collective-permute-start | bytes 393224 | tf_op jit(solution)/shard_map/ppermute | solution.py:224
  9.6 10.0 %collective-permute-start.4 = (bf16[128,1024]{1,0:T(8,128)(2,1)}, bf16[128,1024]{1,0:T(8,128)(2,1)S(1)}, u32[]{:S(2)}, u32[]{:S(2)}) collective-permute-start(bf16[128,1024]{1,0:T(8,128)(2,1)} %refs_0_.1), channel_id=1, source_target_pairs={{0,16},{16,0},{32,48},{48,32},{64,80},{80,64},{96,112},{112,96},{1... | collective-permute-start | bytes 786440 | tf_op jit(solution)/shard_map/ppermute | solution.py:231
  14.9 3.3 %copy-start = (bf16[4,512,2048]{2,1,0:T(8,128)(2,1)}, bf16[4,512,2048]{2,1,0:T(8,128)(2,1)S(1)}, u32[]{:S(2)}) copy-start(bf16[4,512,2048]{2,1,0:T(8,128)(2,1)S(1)} %shard_map.149.refs_10_.xt_ref) | copy-start | bytes 25165828
  18.2 2.5 %collective-permute-start.5 = (bf16[128,1024]{1,0:T(8,128)(2,1)S(1)}, bf16[128,1024]{1,0:T(8,128)(2,1)S(1)}, u32[]{:S(2)}, u32[]{:S(2)}) collective-permute-start(bf16[128,1024]{1,0:T(8,128)(2,1)S(1)} %collective-permute-done.2.refs_1_), channel_id=1, source_target_pairs={{0,16},{16,0},{32,48},{48,32},{64,80},{80,64},{96,112},{112,96},{1... | collective-permute-start | bytes 786440 | tf_op jit(solution)/shard_map/ppermute | solution.py:231
  18.8 1.9 %collective-permute-start.6 = (bf16[128,1024]{1,0:T(8,128)(2,1)S(1)}, bf16[128,1024]{1,0:T(8,128)(2,1)S(1)}, u32[]{:S(2)}, u32[]{:S(2)}) collective-permute-start(bf16[128,1024]{1,0:T(8,128)(2,1)S(1)} %collective-permute-done.3.refs_2_), channel_id=1, source_target_pairs={{0,16},{16,0},{32,48},{48,32},{64,80},{80,64},{96,112},{112,96},{1... | collective-permute-start | bytes 786440 | tf_op jit(solution)/shard_map/ppermute | solution.py:231
  18.9 1.6 %collective-permute-start.7 = (bf16[64,1024]{1,0:T(8,128)(2,1)S(1)}, bf16[64,1024]{1,0:T(8,128)(2,1)S(1)}, u32[]{:S(2)}, u32[]{:S(2)}) collective-permute-start(bf16[64,1024]{1,0:T(8,128)(2,1)S(1)} %collective-permute-done.refs_3_), channel_id=1, source_target_pairs={{0,16},{16,0},{32,48},{48,32},{64,80},{80,64},{96,112},{112,96},{1... | collective-permute-start | bytes 393224 | tf_op jit(solution)/shard_map/ppermute | solution.py:231
  19.3 1.4 %collective-permute-start.8 = (bf16[64,1024]{1,0:T(8,128)(2,1)S(1)}, bf16[64,1024]{1,0:T(8,128)(2,1)S(1)}, u32[]{:S(2)}, u32[]{:S(2)}) collective-permute-start(bf16[64,1024]{1,0:T(8,128)(2,1)S(1)} %collective-permute-done.1.refs_4_), channel_id=1, source_target_pairs={{0,16},{16,0},{32,48},{48,32},{64,80},{80,64},{96,112},{112,96},{1... | collective-permute-start | bytes 393224 | tf_op jit(solution)/shard_map/ppermute | solution.py:231
  20.7 40.1 %slice-start = ((s8[8388608]{0:T(1024)(128)(4,1)}), s8[4194304]{0:T(1024)(128)(4,1)S(1)}, s32[]{:S(2)}) async-start(s8[8388608]{0:T(1024)(128)(4,1)} %bitcast.12), calls=%async_computation.3 | async-start | bytes 8388608
  20.8 40.1 %slice-start.1 = ((s8[8388608]{0:T(1024)(128)(4,1)}), s8[4194304]{0:T(1024)(128)(4,1)S(1)}, s32[]{:S(2)}) async-start(s8[8388608]{0:T(1024)(128)(4,1)} %bitcast.12), calls=%async_computation.4 | async-start | bytes 8388608
  20.8 40.1 %copy-start.1 = (bf16[4,512,2048]{2,1,0:T(8,128)(2,1)S(1)}, bf16[4,512,2048]{2,1,0:T(8,128)(2,1)}, u32[]{:S(2)}) copy-start(bf16[4,512,2048]{2,1,0:T(8,128)(2,1)} %copy-done) | copy-start | bytes 25165828
  32.0 28.9 %copy-start.4 = (bf16[256,256]{1,0:T(8,128)(2,1)S(1)}, bf16[256,256]{1,0:T(8,128)(2,1)}, u32[]{:S(2)}) copy-start(bf16[256,256]{1,0:T(8,128)(2,1)} %w2_ref.1) | copy-start | bytes 393220
  32.0 28.9 %copy-start.7 = (bf16[64,256]{1,0:T(8,128)(2,1)S(1)}, bf16[64,256]{1,0:T(8,128)(2,1)}, u32[]{:S(2)}) copy-start(bf16[64,256]{1,0:T(8,128)(2,1)} %w1_ref.1) | copy-start | bytes 98308
  32.0 28.9 %copy-start.8 = (bf16[256,64]{0,1:T(8,128)(2,1)S(1)}, bf16[256,64]{0,1:T(8,128)(2,1)}, u32[]{:S(2)}) copy-start(bf16[256,64]{0,1:T(8,128)(2,1)} %param.26) | copy-start | bytes 98308
  32.0 28.8 %copy-start.10 = (f32[256]{0:T(256)S(1)}, f32[256]{0:T(256)}, u32[]{:S(2)}) copy-start(f32[256]{0:T(256)} %param.23) | copy-start | bytes 3076
  32.1 28.8 %copy-start.11 = (f32[256]{0:T(256)S(1)}, f32[256]{0:T(256)}, u32[]{:S(2)}) copy-start(f32[256]{0:T(256)} %param.25) | copy-start | bytes 3076
  32.1 28.8 %copy-start.12 = (f32[64]{0:T(128)S(1)}, f32[64]{0:T(128)}, u32[]{:S(2)}) copy-start(f32[64]{0:T(128)} %param.21) | copy-start | bytes 772
  32.1 28.8 %copy-start.13 = (f32[64]{0:T(128)S(1)}, f32[64]{0:T(128)}, u32[]{:S(2)}) copy-start(f32[64]{0:T(128)} %param.27) | copy-start | bytes 772
  69.2 2.7 %collective-permute-start.9 = (bf16[4,8,128,128]{3,2,1,0:T(8,128)(2,1)S(1)}, bf16[4,8,128,128]{3,2,1,0:T(8,128)(2,1)S(1)}, u32[]{:S(2)}, u32[]{:S(2)}) collective-permute-start(bf16[4,8,128,128]{3,2,1,0:T(8,128)(2,1)S(1)} %get-tuple-element.20), channel_id=1, source_target_pairs={{0,16},{16,0},{32,48},{48,32},{64,80},{80,64},{96,112},{112,96},{1... | collective-permute-start | bytes 3145736 | tf_op jit(solution)/shard_map/ppermute | solution.py:322

commit v2 on v1

--- a/solution.py
+++ b/solution.py
@@ -64,22 +64,15 @@
     )(x)
 
 
-def slab_copies(pos_ref, chips, slabs, table_ref, sem_ref):
+def place_slabs(pos_ref, chips, slabs, table_ref):
     core, z = pos_ref[0], pos_ref[2]
     half = table_ref.shape[1] // 2
-    top, bottom = pl.ds(0, half), pl.ds(half, half)
-    every = pl.ds(0, 2 * half)
-    places = [(0, every), (chips - 1, every), (1, every), (2, top), (2, bottom)]
-    copies = []
+    places = [(0, 0), (chips - 1, 0), (1, 0), (2, 0), (2, half)]
     for side in range(2):
-        for k, (shift, rows) in enumerate(places):
-            chip = lax.rem(z + shift, chips)
-            slot = 2 * chip + (core if side == 0 else 1 - core)
-            n = side * len(places) + k
-            copies.append(
-                pltpu.make_async_copy(slabs[n], table_ref.at[slot, rows], sem_ref.at[n])
-            )
-    return copies
+        for k, (shift, start) in enumerate(places):
+            slot = 2 * lax.rem(z + shift, chips) + (core if side == 0 else 1 - core)
+            slab = slabs[side * len(places) + k]
+            table_ref[slot, start : start + slab.shape[0], :] = slab[...]
 
 
 def density_kernel(
@@ -90,52 +83,44 @@
 
 
 def density_body(
-    tile, chunk, chips, tid_ref, pos_ref, slabs, xt_ref, desc_ref, w_ref, ids_ref, scale_ref,
-    dens_ref, sum_ref, table_ref, panel_ref, acc_ref, sem_ref,
+    tile, chunk, chips, tid_ref, pos_ref, slabs, x_ref, desc_ref, w_ref, ids_ref, scale_ref,
+    dens_ref, sum_ref, table_ref, panel_ref, acc_ref,
 ):
-    b, part = pl.program_id(0), pl.program_id(1)
-    parts = pl.num_programs(1)
-    orbitals, points = xt_ref.shape[1:]
+    b = pl.program_id(0)
+    points, orbitals = x_ref.shape[1:]
     per_batch = orbitals // tile
     feats = desc_ref.shape[1]
     centres = sum_ref.shape[2]
 
-    @pl.when((b == 0) & (part == 0))
+    @pl.when(b == 0)
     def _():
-        copies = slab_copies(pos_ref, chips, slabs, table_ref, sem_ref)
-        for copy in copies:
-            copy.start()
-        for copy in copies:
-            copy.wait()
-
-    @pl.when(part == 0)
-    def _():
-        for i in range(per_batch):
-            ti = tid_ref[b, i]
-            for j in range(per_batch):
-                tj = tid_ref[b, j]
-                panel_ref[i * tile : (i + 1) * tile, j * tile : (j + 1) * tile] = table_ref[
-                    ti, :, pl.ds(pl.multiple_of(tj * tile, tile), tile)
-                ]
+        place_slabs(pos_ref, chips, slabs, table_ref)
+
+    for i in range(per_batch):
+        ti = tid_ref[b, i]
+        for j in range(per_batch):
+            tj = tid_ref[b, j]
+            panel_ref[i * tile : (i + 1) * tile, j * tile : (j + 1) * tile] = table_ref[
+                ti, :, pl.ds(pl.multiple_of(tj * tile, tile), tile)
+            ]
 
     gathered = jnp.zeros(acc_ref.shape[1:], F32)
     for r in range(points // chunk):
         at = slice(r * chunk, (r + 1) * chunk)
-        out = pl.ds(pl.multiple_of(part * points + r * chunk, chunk), chunk)
-        xt = xt_ref[0, :, at]
+        xt = x_ref[0, at, :].T
         q = jnp.dot(panel_ref[...], xt, preferred_element_type=F32)
         dens = jnp.sum(xt.astype(F32) * q, axis=0, keepdims=True)
-        dens_ref[pl.ds(b, 1), out] = dens
+        dens_ref[pl.ds(b, 1), at] = dens
         f = silu(dens * scale_ref[...] + desc_ref[0, :, at].astype(F32))
-        f = f * w_ref[pl.ds(b, 1), out]
+        f = f * w_ref[pl.ds(b, 1), at]
         high = f.astype(BF)
         low = (f - high.astype(F32)).astype(BF)
         both = jnp.concatenate([high, low], axis=0)
-        hot = one_hot(ids_ref[pl.ds(b, 1), out], centres)
+        hot = one_hot(ids_ref[pl.ds(b, 1), at], centres)
         gathered += lax.dot_general(both, hot, LANES, preferred_element_type=F32)
-    acc_ref[b * parts + part] = gathered
-
-    @pl.when((b == pl.num_programs(0) - 1) & (part == parts - 1))
+    acc_ref[b] = gathered
+
+    @pl.when(b == pl.num_programs(0) - 1)
     def _():
         total = jnp.sum(acc_ref[...], axis=0)
         total = (total[:feats] + total[feats:]).astype(sum_ref.dtype)
@@ -208,7 +193,6 @@
     mine = CENT_DEV
     centres = mine * columns
     chunk = 512
-    parts = 1
     here, there = lax.axis_index("mat"), lax.axis_index("pts")
     pos = jnp.stack([here % 2, there, here // 2]).astype(jnp.int32)
     swap = [(i, i ^ 1) for i in range(mats)]
@@ -234,11 +218,11 @@
         functools.partial(density_kernel, tile, chunk, chips),
         grid_spec=pltpu.PrefetchScalarGridSpec(
             num_scalar_prefetch=2,
-            grid=(batches, parts),
+            grid=(batches,),
             in_specs=[
-                *[pl.BlockSpec(memory_space=pl.ANY)] * len(slabs),
-                pl.BlockSpec((1, orbitals, points // parts), lambda b, r, *_: (b, 0, r)),
-                pl.BlockSpec((1, feats, points // parts), lambda b, r, *_: (b, 0, r)),
+                *[whole(slab.shape) for slab in slabs],
+                pl.BlockSpec((1, points, orbitals), lambda b, *_: (b, 0, 0)),
+                pl.BlockSpec((1, feats, points), lambda b, *_: (b, 0, 0)),
                 whole((batches, points)),
                 whole((batches, points)),
                 whole((feats, 1)),
@@ -247,8 +231,7 @@
             scratch_shapes=[
                 pltpu.VMEM((tiles, tile, basis), BF),
                 pltpu.VMEM((orbitals, orbitals), BF),
-                pltpu.VMEM((batches * parts, 2 * feats, centres), F32),
-                pltpu.SemaphoreType.DMA((len(slabs),)),
+                pltpu.VMEM((batches, 2 * feats, centres), F32),
             ],
         ),
         out_shape=[
@@ -261,7 +244,9 @@
             bytes_accessed=2 * basis_values.size,
             transcendentals=descriptors.size,
         ),
-    )(tile_ids, pos, *slabs, in_hbm(xt), desc, grid_weights, centre_ids, scale)
+    )(
+        tile_ids, pos, *slabs, in_hbm(basis_values), desc, grid_weights, centre_ids, scale,
+    )
 
     first = summed(lax.all_to_all(partial, "mat", 0, 0, tiled=True), (columns,))
     sums = lax.all_to_all(first, "pts", 0, 0, tiled=True)

time: 96.9 us -> 96.2 us (level)
  transfers between devices with their start and end apart: 10 -> 10, of which waited for: 3 -> 3; matrix products, arithmetic and copies ran while one was open for 1% -> 1% of each run, Pallas kernels for 5% -> 6%
where the time goes in v2:
time: 96.2 us; the launch traced here: 95.9 us
  blocking collectives  52.4 us (54%)
  Pallas kernels  24.9 us (26%)
  starting transfers between devices  9.16 us (10%)
  local copies, waits for them, and re-layouts  4.43 us (5%)
  waiting for transfers between devices  3.81 us (4%)
    all_to_all x1, blocking collectives, shards(): lax.all_to_all(joined, ('mat', 'pts'), 0, 0, tiled=True, axis_index_group...  23.7 us
    all_to_all x1, blocking collectives, shards(): sums = lax.all_to_all(first, 'pts', 0, 0, tiled=True)  18 us
    all_to_all x1, blocking collectives, shards(): first = summed(lax.all_to_all(partial, 'mat', 0, 0, tiled=True), (columns,))  10.7 us
    pallas_call x1, Pallas kernels, shards(): pl.pallas_call(functools.partial(density_kernel, tile, chunk, chips), gri...  10.4 us
    pallas_call x1, Pallas kernels, shards(): pl.pallas_call(functools.partial(potential_kernel, tile, chunk, factor),...  8.29 us
    pallas_call x1, Pallas kernels, transposed(): pl.pallas_call(transpose_kernel, grid=(batches, points // chunk), in_spec...  5.29 us
    unnamed x34, local copies, waits for them, and re-layouts  3.35 us
    ppermute x1, waiting for transfers between devices, shards(): joined = (own + lax.ppermute(other, 'mat', swap).astype(F32)).astype(BF)  2.66 us
  transfers between devices with their start and end apart: 10, of which 3 were waited for; matrix products, arithmetic and copies ran while one was open for 1% of the time, Pallas kernels for 6%

profile of v2, /device:TPU:0, one launch (start us, length us, event | category | flops | bytes accessed | tf_op | source)
XLA Modules:
  0.0 95.9 jit_solution(2644223615981994790)
XLA Ops:
  0.6 2.1 %collective-permute-start.2 = (bf16[128,1024]{1,0:T(8,128)(2,1)}, bf16[128,1024]{1,0:T(8,128)(2,1)S(1)}, u32[]{:S(2)}, u32[]{:S(2)}) collective-permute-start(bf16[128,1024]{1,0:T(8,128)(2,1)} %refs_0_.1), channel_id=1, source_target_pairs={{0,32},{16,48},{32,64},{48,80},{64,96},{80,112},{96,0},{112,16},{1... | collective-permute-start | bytes 786440 | tf_op jit(solution)/shard_map/ppermute | solution.py:210
  2.7 2.2 %collective-permute-start.3 = (bf16[128,1024]{1,0:T(8,128)(2,1)}, bf16[128,1024]{1,0:T(8,128)(2,1)S(1)}, u32[]{:S(2)}, u32[]{:S(2)}) collective-permute-start(bf16[128,1024]{1,0:T(8,128)(2,1)} %refs_0_.1), channel_id=1, source_target_pairs={{0,96},{16,112},{32,0},{48,16},{64,32},{80,48},{96,64},{112,80},{1... | collective-permute-start | bytes 786440 | tf_op jit(solution)/shard_map/ppermute | solution.py:211
  4.9 1.0 %fusion = (bf16[64,1024]{1,0:T(8,128)(2,1)S(1)}, bf16[64,1024]{1,0:T(8,128)(2,1)S(1)}) fusion(bf16[128,1024]{1,0:T(8,128)(2,1)} %refs_0_.1), kind=kLoop, calls=%fused_computation.2 | loop fusion | bytes 524288 | tf_op jit(solution)/shard_map/slice | solution.py:209
  5.9 1.9 %collective-permute-start.1 = (bf16[64,1024]{1,0:T(8,128)(2,1)S(1)}, bf16[64,1024]{1,0:T(8,128)(2,1)S(1)}, u32[]{:S(2)}, u32[]{:S(2)}) collective-permute-start(bf16[64,1024]{1,0:T(8,128)(2,1)S(1)} %get-tuple-element.22), channel_id=1, source_target_pairs={{0,64},{16,80},{32,96},{48,112},{64,0},{80,16},{96,32},{112,48},{1... | collective-permute-start | bytes 393224 | tf_op jit(solution)/shard_map/ppermute | solution.py:209
  7.8 0.0 copy-start.2
  7.8 0.0 copy-start.3
  7.8 0.0 copy-start.5
  7.8 0.0 copy-start.6
  7.8 0.0 copy-start.9
  7.8 1.8 %collective-permute-start = (bf16[64,1024]{1,0:T(8,128)(2,1)S(1)}, bf16[64,1024]{1,0:T(8,128)(2,1)S(1)}, u32[]{:S(2)}, u32[]{:S(2)}) collective-permute-start(bf16[64,1024]{1,0:T(8,128)(2,1)S(1)} %get-tuple-element.23), channel_id=1, source_target_pairs={{0,64},{16,80},{32,96},{48,112},{64,0},{80,16},{96,32},{112,48},{1... | collective-permute-start | bytes 393224 | tf_op jit(solution)/shard_map/ppermute | solution.py:208
  9.6 0.0 collective-permute-start.4
  9.6 5.3 %shard_map.149.xt_ref = bf16[4,512,2048]{2,1,0:T(8,128)(2,1)S(1)} custom-call(bf16[4,2048,512]{2,1,0:T(8,128)(2,1)} %x_ref.3), custom_call_target="tpu_custom_call" | custom-call | bytes 16777216 | tf_op jit(solution)/shard_map/pallas_call | solution.py:41
  14.9 0.0 copy-start
  14.9 3.3 %copy-done = bf16[4,512,2048]{2,1,0:T(8,128)(2,1)} copy-done((bf16[4,512,2048]{2,1,0:T(8,128)(2,1)}, bf16[4,512,2048]{2,1,0:T(8,128)(2,1)S(1)}, u32[]{:S(2)}) %copy-start) | copy-done | bytes 8388632
  18.2 0.0 collective-permute-done.1.refs_4_
  18.2 0.0 collective-permute-done.refs_3_
  18.2 0.0 collective-permute-done.2.refs_1_
  18.2 0.0 collective-permute-done.3.refs_2_
  18.2 0.6 collective-permute-start.5
  18.8 0.1 collective-permute-start.6
  18.9 0.4 collective-permute-start.7
  19.3 0.1 collective-permute-start.8
  19.4 0.0 copy-done.14
  19.4 0.1 copy.16.refs_14_
  19.5 0.1 pad_add_fusion.pos_ref
  19.6 0.0 collective-permute-done.4.refs_5_
  19.6 0.9 collective-permute-done.7.refs_8_
  20.5 0.2 collective-permute-done.8.refs_9_
  20.7 0.0 collective-permute-done.5.refs_6_
  20.7 0.0 collective-permute-done.6.refs_7_
  20.7 0.0 copy-done.2
  20.7 0.0 copy-done.3
  20.8 0.0 copy-done.5
  20.8 0.0 copy-done.6
  20.8 0.0 copy-done.9
  20.8 0.0 slice-start.1
  20.8 0.0 copy-start.1
  20.8 10.4 %shard_map.150 = (f32[4,2048]{1,0:T(4,128)S(1)}, bf16[8,64,256]{2,1,0:T(8,128)(2,1)S(1)}) custom-call(s32[4,4]{1,0:T(4,128)S(1)} %copy-done.9, s32[3]{0:T(128)S(1)} %pad_add_fusion.pos_ref, bf16[128,1024]{1,0:T(8,128)(2,1)S(1)} %copy-done.3, bf16[128,1024]{1,0:T(8,128)(2,1)S(1)} %collective-permute-done.2.refs_1_, ...), custom_call_target="tpu_custom_call" | custom-call | flops 4294967296 | bytes 8388608 | tf_op jit(solution)/shard_map/pallas_call | solution.py:217
  31.3 0.0 copy-start.4
  31.3 0.0 copy-start.7
  31.3 0.0 copy-start.8
  31.3 0.0 copy-start.10
  31.3 0.0 copy-start.11
  31.3 0.0 copy-start.12
  31.3 0.0 copy-start.13
  31.3 10.7 %all_to_all.15.x_ref = bf16[8,64,256]{2,1,0:T(8,128)(2,1)S(1)} all-to-all(bf16[8,64,256]{2,1,0:T(8,128)(2,1)S(1)} %get-tuple-element.16), channel_id=1, replica_groups=mesh['mat'=8,'pts'=16] {'mat'}, dimensions={0} | all-to-all | bytes 524288 | tf_op jit(solution)/shard_map/all_to_all | solution.py:251
  42.0 0.1 shard_map.151
  42.1 18.0 %all_to_all.16.sums_ref = bf16[16,64,256]{2,1,0:T(8,128)(2,1)S(1)} all-to-all(bf16[16,64,256]{2,1,0:T(8,128)(2,1)S(1)} %shard_map.151), channel_id=1, replica_groups=mesh['mat'=8,'pts'=16] {'pts'}, dimensions={0} | all-to-all | bytes 1048576 | tf_op jit(solution)/shard_map/all_to_all | solution.py:252
  60.1 0.0 slice-done
  60.1 0.0 slice-done.1
  60.1 0.0 copy-done.1
  60.1 0.0 copy-done.4
  60.1 0.0 copy-done.7
  60.1 0.0 copy-done.8
  60.1 0.0 copy-done.10
  60.2 0.0 copy-done.11
  60.2 0.0 copy-done.12
  60.2 0.0 copy-done.13
  60.2 8.3 %shard_map.152 = (f32[4,8,128,128]{3,2,1,0:T(8,128)S(1)}, bf16[4,8,128,128]{3,2,1,0:T(8,128)(2,1)S(1)}, bf16[16,64]{1,0:T(8,128)(2,1)}) custom-call(s32[4,4]{1,0:T(4,128)S(1)} %copy-done.9, s32[3]{0:T(128)S(1)} %pad_add_fusion.pos_ref, bf16[16,64,256]{2,1,0:T(8,128)(2,1)S(1)} %all_to_all.16.sums_ref, f32[1,64]{1,0:T(1,128)S(1)} %bitcast.19, ...), custom_call_target="tpu_custom_call" | custom-call | flops 4294967296 | bytes 16777216 | tf_op jit(solution)/shard_map/pallas_call | solution.py:257
  68.5 0.0 collective-permute-start.9
  68.5 2.7 %collective-permute-done.9 = bf16[4,8,128,128]{3,2,1,0:T(8,128)(2,1)S(1)} collective-permute-done((bf16[4,8,128,128]{3,2,1,0:T(8,128)(2,1)S(1)}, bf16[4,8,128,128]{3,2,1,0:T(8,128)(2,1)S(1)}, u32[]{:S(2)}, u32[]{:S(2)}) %collective-permute-start.9) | collective-permute-done | bytes 1048608 | tf_op jit(solution)/shard_map/ppermute | solution.py:307
  71.2 0.3 add_convert_fusion
  71.5 23.7 %all_to_all.17.x_ref = bf16[64,64,128]{2,1,0:T(8,128)(2,1)S(1)} all-to-all(bf16[64,64,128]{2,1,0:T(8,128)(2,1)S(1)} %bitcast.21), channel_id=1, replica_groups={{0,1,2,3,4,5,6,7,8,9,10,11,12,13,14,15,32,33,34,35,36,37,38,39,40,41,42..., dimensions={0} | all-to-all | bytes 2097152 | tf_op jit(solution)/shard_map/all_to_all | solution.py:309
  95.1 0.8 shard_map.153
  (3 shorter events, 0.0 us)
Async XLA Ops:
  0.6 17.6 %collective-permute-start.2 = (bf16[128,1024]{1,0:T(8,128)(2,1)}, bf16[128,1024]{1,0:T(8,128)(2,1)S(1)}, u32[]{:S(2)}, u32[]{:S(2)}) collective-permute-start(bf16[128,1024]{1,0:T(8,128)(2,1)} %refs_0_.1), channel_id=1, source_target_pairs={{0,32},{16,48},{32,64},{48,80},{64,96},{80,112},{96,0},{112,16},{1... | collective-permute-start | bytes 786440 | tf_op jit(solution)/shard_map/ppermute | solution.py:210
  2.7 15.5 %collective-permute-start.3 = (bf16[128,1024]{1,0:T(8,128)(2,1)}, bf16[128,1024]{1,0:T(8,128)(2,1)S(1)}, u32[]{:S(2)}, u32[]{:S(2)}) collective-permute-start(bf16[128,1024]{1,0:T(8,128)(2,1)} %refs_0_.1), channel_id=1, source_target_pairs={{0,96},{16,112},{32,0},{48,16},{64,32},{80,48},{96,64},{112,80},{1... | collective-permute-start | bytes 786440 | tf_op jit(solution)/shard_map/ppermute | solution.py:211
  5.9 12.3 %collective-permute-start.1 = (bf16[64,1024]{1,0:T(8,128)(2,1)S(1)}, bf16[64,1024]{1,0:T(8,128)(2,1)S(1)}, u32[]{:S(2)}, u32[]{:S(2)}) collective-permute-start(bf16[64,1024]{1,0:T(8,128)(2,1)S(1)} %get-tuple-element.22), channel_id=1, source_target_pairs={{0,64},{16,80},{32,96},{48,112},{64,0},{80,16},{96,32},{112,48},{1... | collective-permute-start | bytes 393224 | tf_op jit(solution)/shard_map/ppermute | solution.py:209
  7.8 11.7 %copy-start.14 = (f32[64]{0:T(128)S(1)}, f32[64]{0:T(128)}, u32[]{:S(2)}) copy-start(f32[64]{0:T(128)} %param.20) | copy-start | bytes 772
  7.8 13.0 %copy-start.2 = (bf16[4,2048,64]{1,2,0:T(8,128)(2,1)S(1)}, bf16[4,2048,64]{1,2,0:T(8,128)(2,1)}, u32[]{:S(2)}) copy-start(bf16[4,2048,64]{1,2,0:T(8,128)(2,1)} %param.17) | copy-start | bytes 3145732
  7.8 13.0 %copy-start.3 = (bf16[128,1024]{1,0:T(8,128)(2,1)S(1)}, bf16[128,1024]{1,0:T(8,128)(2,1)}, u32[]{:S(2)}) copy-start(bf16[128,1024]{1,0:T(8,128)(2,1)} %refs_0_.1) | copy-start | bytes 786436
  7.8 13.0 %copy-start.5 = (f32[4,2048]{1,0:T(4,128)S(1)}, f32[4,2048]{1,0:T(4,128)}, u32[]{:S(2)}) copy-start(f32[4,2048]{1,0:T(4,128)} %w_ref.1) | copy-start | bytes 98308
  7.8 13.0 %copy-start.6 = (s32[4,2048]{1,0:T(4,128)S(1)}, s32[4,2048]{1,0:T(4,128)}, u32[]{:S(2)}) copy-start(s32[4,2048]{1,0:T(4,128)} %ids_ref.1) | copy-start | bytes 98308
  7.8 13.0 %copy-start.9 = (s32[4,4]{1,0:T(4,128)S(1)}, s32[4,4]{1,0:T(4,128)}, u32[]{:S(2)}) copy-start(s32[4,4]{1,0:T(4,128)} %tid_ref.3) | copy-start | bytes 196
  7.8 10.4 %collective-permute-start = (bf16[64,1024]{1,0:T(8,128)(2,1)S(1)}, bf16[64,1024]{1,0:T(8,128)(2,1)S(1)}, u32[]{:S(2)}, u32[]{:S(2)}) collective-permute-start(bf16[64,1024]{1,0:T(8,128)(2,1)S(1)} %get-tuple-element.23), channel_id=1, source_target_pairs={{0,64},{16,80},{32,96},{48,112},{64,0},{80,16},{96,32},{112,48},{1... | collective-permute-start | bytes 393224 | tf_op jit(solution)/shard_map/ppermute | solution.py:208
  9.6 10.0 %collective-permute-start.4 = (bf16[128,1024]{1,0:T(8,128)(2,1)}, bf16[128,1024]{1,0:T(8,128)(2,1)S(1)}, u32[]{:S(2)}, u32[]{:S(2)}) collective-permute-start(bf16[128,1024]{1,0:T(8,128)(2,1)} %refs_0_.1), channel_id=1, source_target_pairs={{0,16},{16,0},{32,48},{48,32},{64,80},{80,64},{96,112},{112,96},{1... | collective-permute-start | bytes 786440 | tf_op jit(solution)/shard_map/ppermute | solution.py:215
  14.9 3.3 %copy-start = (bf16[4,512,2048]{2,1,0:T(8,128)(2,1)}, bf16[4,512,2048]{2,1,0:T(8,128)(2,1)S(1)}, u32[]{:S(2)}) copy-start(bf16[4,512,2048]{2,1,0:T(8,128)(2,1)S(1)} %shard_map.149.xt_ref) | copy-start | bytes 25165828
  18.2 2.5 %collective-permute-start.5 = (bf16[128,1024]{1,0:T(8,128)(2,1)S(1)}, bf16[128,1024]{1,0:T(8,128)(2,1)S(1)}, u32[]{:S(2)}, u32[]{:S(2)}) collective-permute-start(bf16[128,1024]{1,0:T(8,128)(2,1)S(1)} %collective-permute-done.2.refs_1_), channel_id=1, source_target_pairs={{0,16},{16,0},{32,48},{48,32},{64,80},{80,64},{96,112},{112,96},{1... | collective-permute-start | bytes 786440 | tf_op jit(solution)/shard_map/ppermute | solution.py:215
  18.8 1.9 %collective-permute-start.6 = (bf16[128,1024]{1,0:T(8,128)(2,1)S(1)}, bf16[128,1024]{1,0:T(8,128)(2,1)S(1)}, u32[]{:S(2)}, u32[]{:S(2)}) collective-permute-start(bf16[128,1024]{1,0:T(8,128)(2,1)S(1)} %collective-permute-done.3.refs_2_), channel_id=1, source_target_pairs={{0,16},{16,0},{32,48},{48,32},{64,80},{80,64},{96,112},{112,96},{1... | collective-permute-start | bytes 786440 | tf_op jit(solution)/shard_map/ppermute | solution.py:215
  18.9 1.6 %collective-permute-start.7 = (bf16[64,1024]{1,0:T(8,128)(2,1)S(1)}, bf16[64,1024]{1,0:T(8,128)(2,1)S(1)}, u32[]{:S(2)}, u32[]{:S(2)}) collective-permute-start(bf16[64,1024]{1,0:T(8,128)(2,1)S(1)} %collective-permute-done.refs_3_), channel_id=1, source_target_pairs={{0,16},{16,0},{32,48},{48,32},{64,80},{80,64},{96,112},{112,96},{1... | collective-permute-start | bytes 393224 | tf_op jit(solution)/shard_map/ppermute | solution.py:215
  19.3 1.4 %collective-permute-start.8 = (bf16[64,1024]{1,0:T(8,128)(2,1)S(1)}, bf16[64,1024]{1,0:T(8,128)(2,1)S(1)}, u32[]{:S(2)}, u32[]{:S(2)}) collective-permute-start(bf16[64,1024]{1,0:T(8,128)(2,1)S(1)} %collective-permute-done.1.refs_4_), channel_id=1, source_target_pairs={{0,16},{16,0},{32,48},{48,32},{64,80},{80,64},{96,112},{112,96},{1... | collective-permute-start | bytes 393224 | tf_op jit(solution)/shard_map/ppermute | solution.py:215
  20.7 39.4 %slice-start = ((s8[8388608]{0:T(1024)(128)(4,1)}), s8[4194304]{0:T(1024)(128)(4,1)S(1)}, s32[]{:S(2)}) async-start(s8[8388608]{0:T(1024)(128)(4,1)} %bitcast.12), calls=%async_computation.3 | async-start | bytes 8388608
  20.8 39.3 %slice-start.1 = ((s8[8388608]{0:T(1024)(128)(4,1)}), s8[4194304]{0:T(1024)(128)(4,1)S(1)}, s32[]{:S(2)}) async-start(s8[8388608]{0:T(1024)(128)(4,1)} %bitcast.12), calls=%async_computation.4 | async-start | bytes 8388608
  20.8 39.3 %copy-start.1 = (bf16[4,512,2048]{2,1,0:T(8,128)(2,1)S(1)}, bf16[4,512,2048]{2,1,0:T(8,128)(2,1)}, u32[]{:S(2)}) copy-start(bf16[4,512,2048]{2,1,0:T(8,128)(2,1)} %copy-done) | copy-start | bytes 25165828
  31.3 28.9 %copy-start.4 = (bf16[256,256]{1,0:T(8,128)(2,1)S(1)}, bf16[256,256]{1,0:T(8,128)(2,1)}, u32[]{:S(2)}) copy-start(bf16[256,256]{1,0:T(8,128)(2,1)} %w2_ref.1) | copy-start | bytes 393220
  31.3 28.9 %copy-start.7 = (bf16[64,256]{1,0:T(8,128)(2,1)S(1)}, bf16[64,256]{1,0:T(8,128)(2,1)}, u32[]{:S(2)}) copy-start(bf16[64,256]{1,0:T(8,128)(2,1)} %w1_ref.1) | copy-start | bytes 98308
  31.3 28.9 %copy-start.8 = (bf16[256,64]{0,1:T(8,128)(2,1)S(1)}, bf16[256,64]{0,1:T(8,128)(2,1)}, u32[]{:S(2)}) copy-start(bf16[256,64]{0,1:T(8,128)(2,1)} %param.26) | copy-start | bytes 98308
  31.3 28.9 %copy-start.10 = (f32[256]{0:T(256)S(1)}, f32[256]{0:T(256)}, u32[]{:S(2)}) copy-start(f32[256]{0:T(256)} %param.23) | copy-start | bytes 3076
  31.3 28.9 %copy-start.11 = (f32[256]{0:T(256)S(1)}, f32[256]{0:T(256)}, u32[]{:S(2)}) copy-start(f32[256]{0:T(256)} %param.25) | copy-start | bytes 3076
  31.3 28.9 %copy-start.12 = (f32[64]{0:T(128)S(1)}, f32[64]{0:T(128)}, u32[]{:S(2)}) copy-start(f32[64]{0:T(128)} %param.21) | copy-start | bytes 772
  31.3 28.9 %copy-start.13 = (f32[64]{0:T(128)S(1)}, f32[64]{0:T(128)}, u32[]{:S(2)}) copy-start(f32[64]{0:T(128)} %param.27) | copy-start | bytes 772
  68.5 2.7 %collective-permute-start.9 = (bf16[4,8,128,128]{3,2,1,0:T(8,128)(2,1)S(1)}, bf16[4,8,128,128]{3,2,1,0:T(8,128)(2,1)S(1)}, u32[]{:S(2)}, u32[]{:S(2)}) collective-permute-start(bf16[4,8,128,128]{3,2,1,0:T(8,128)(2,1)S(1)} %get-tuple-element.20), channel_id=1, source_target_pairs={{0,16},{16,0},{32,48},{48,32},{64,80},{80,64},{96,112},{112,96},{1... | collective-permute-start | bytes 3145736 | tf_op jit(solution)/shard_map/ppermute | solution.py:307

commit v3 on v2

--- a/solution.py
+++ b/solution.py
@@ -56,10 +56,10 @@
     o_ref[...] = jnp.broadcast_to(total, o_ref.shape)
 
 
-def summed(x, copies=()):
+def summed(x, copies=(), kind=BF):
     return pl.pallas_call(
         sum_kernel,
-        out_shape=jax.ShapeDtypeStruct((*copies, *x.shape[1:]), x.dtype),
+        out_shape=jax.ShapeDtypeStruct((*copies, *x.shape[1:]), kind),
         compiler_params=pltpu.CompilerParams(vmem_limit_bytes=8 * MB),
     )(x)
 
@@ -90,7 +90,7 @@
     points, orbitals = x_ref.shape[1:]
     per_batch = orbitals // tile
     feats = desc_ref.shape[1]
-    centres = sum_ref.shape[2]
+    centres = 2 * sum_ref.shape[2]
 
     @pl.when(b == 0)
     def _():
@@ -124,11 +124,13 @@
     def _():
         total = jnp.sum(acc_ref[...], axis=0)
         total = (total[:feats] + total[feats:]).astype(sum_ref.dtype)
-        sum_ref[...] = jnp.broadcast_to(total, sum_ref.shape)
+        side = sum_ref.shape[2]
+        for m in range(sum_ref.shape[0]):
+            sum_ref[m] = total[:, (m % 2) * side : (m % 2 + 1) * side]
 
 
 def potential_kernel(
-    tile, chunk, factor, tid_ref, pos_ref, sums_ref, gain_ref, w1_ref, b1_ref, w2_ref, b2_ref, w3_ref,
+    tile, chunk, factor, tid_ref, pos_ref, sum_ref, sum_ref_too, gain_ref, w1_ref, b1_ref, w2_ref, b2_ref, w3_ref,
     b3_ref, dens_ref, desc_ref, w_ref, ids_ref, xt_ref, x_ref, own_ref, other_ref, cf_ref,
     cft_ref, cfall_ref, wt_ref, acc_ref,
 ):
@@ -141,7 +143,11 @@
     @pl.when(b == 0)
     def _():
         acc_ref[...] = jnp.zeros_like(acc_ref)
-        total = jnp.sum(sums_ref[...].astype(F32), axis=0)
+        even = pos_ref[0] == 0
+        here, there = sum_ref[...], sum_ref_too[...]
+        total = jnp.concatenate(
+            [jnp.where(even, here, there), jnp.where(even, there, here)], axis=1
+        )
         inverse = lax.rsqrt(jnp.mean(total * total, axis=0, keepdims=True) + 1e-05)
         normed = ((total * inverse).T * gain_ref[...]).astype(BF)
         one = silu(
@@ -227,7 +233,7 @@
                 whole((batches, points)),
                 whole((feats, 1)),
             ],
-            out_specs=[whole((batches, points)), whole((mats, feats, centres))],
+            out_specs=[whole((batches, points)), whole((mats, feats, centres // 2))],
             scratch_shapes=[
                 pltpu.VMEM((tiles, tile, basis), BF),
                 pltpu.VMEM((orbitals, orbitals), BF),
@@ -236,7 +242,7 @@
         ),
         out_shape=[
             jax.ShapeDtypeStruct((batches, points), F32),
-            jax.ShapeDtypeStruct((mats, feats, centres), BF),
+            jax.ShapeDtypeStruct((mats, feats, centres // 2), BF),
         ],
         compiler_params=pltpu.CompilerParams(vmem_limit_bytes=16 * MB),
         cost_estimate=pl.CostEstimate(
@@ -249,7 +255,8 @@
     )
 
     first = summed(lax.all_to_all(partial, "mat", 0, 0, tiled=True), (columns,))
-    sums = lax.all_to_all(first, "pts", 0, 0, tiled=True)
+    mine_sum = summed(lax.all_to_all(first, "pts", 0, 0, tiled=True), kind=F32)
+    their_sum = lax.ppermute(mine_sum, "mat", swap)
 
     all_batches = batches * mats * columns
     factor = tiles / (per_batch * math.sqrt(points * feats * all_batches))
@@ -260,7 +267,8 @@
             num_scalar_prefetch=2,
             grid=(batches,),
             in_specs=[
-                whole((columns, feats, centres)),
+                whole((feats, centres // 2)),
+                whole((feats, centres // 2)),
                 whole((1, feats)),
                 whole((feats, hidden)),
                 whole((1, hidden)),
@@ -299,7 +307,7 @@
             transcendentals=2 * centres * hidden,
         ),
     )(
-        tile_ids, pos, sums, norm_gain.reshape(1, feats), w_first, b_first.reshape(1, hidden),
+        tile_ids, pos, mine_sum, their_sum, norm_gain.reshape(1, feats), w_first, b_first.reshape(1, hidden),
         w_second, b_second.reshape(1, hidden), w_third.T, b_third.reshape(1, feats), density, desc,
         grid_weights, centre_ids, xt, basis_values,
     )

time: 96.2 us -> 93.5 us (0.972)
  blocking collectives: 52.4 us -> 48.3 us
  waiting for transfers between devices: 3.81 us -> 4.85 us
    all_to_all x1, blocking collectives: 18 us -> 15.5 us  [shards(): mine_sum = summed(lax.all_to_all(first, 'pts', 0, 0, tiled=True), kind=F32)]
    all_to_all x1, blocking collectives: 10.7 us -> 9.17 us  [shards(): first = summed(lax.all_to_all(partial, 'mat', 0, 0, tiled=True), (columns,))]
    ppermute x0 -> x1, waiting for transfers between devices: none -> 1.19 us  [shards(): their_sum = lax.ppermute(mine_sum, 'mat', swap)]
  transfers between devices with their start and end apart: 10 -> 11, of which waited for: 3 -> 4; matrix products, arithmetic and copies ran while one was open for 1% -> 1% of each run, Pallas kernels for 6% -> 6%
where the time goes in v3:
time: 93.5 us; the launch traced here: 93.2 us
  blocking collectives  48.3 us (52%)
  Pallas kernels  25 us (27%)
  starting transfers between devices  9.39 us (10%)
  waiting for transfers between devices  4.85 us (5%)
  local copies, waits for them, and re-layouts  4.43 us (5%)
    all_to_all x1, blocking collectives, shards(): lax.all_to_all(joined, ('mat', 'pts'), 0, 0, tiled=True, axis_index_group...  23.6 us
    all_to_all x1, blocking collectives, shards(): mine_sum = summed(lax.all_to_all(first, 'pts', 0, 0, tiled=True), kind=F32)  15.5 us
    pallas_call x1, Pallas kernels, shards(): pl.pallas_call(functools.partial(density_kernel, tile, chunk, chips), gri...  10.5 us
    all_to_all x1, blocking collectives, shards(): first = summed(lax.all_to_all(partial, 'mat', 0, 0, tiled=True), (columns,))  9.17 us
    pallas_call x1, Pallas kernels, shards(): pl.pallas_call(functools.partial(potential_kernel, tile, chunk, factor),...  8.3 us
    pallas_call x1, Pallas kernels, transposed(): pl.pallas_call(transpose_kernel, grid=(batches, points // chunk), in_spec...  5.29 us
    unnamed x34, local copies, waits for them, and re-layouts  3.34 us
    ppermute x1, waiting for transfers between devices, shards(): joined = (own + lax.ppermute(other, 'mat', swap).astype(F32)).astype(BF)  2.5 us
  transfers between devices with their start and end apart: 11, of which 4 were waited for; matrix products, arithmetic and copies ran while one was open for 1% of the time, Pallas kernels for 6%

profile of v3, /device:TPU:0, one launch (start us, length us, event | category | flops | bytes accessed | tf_op | source)
XLA Modules:
  0.0 93.2 jit_solution(4888458282387221144)
XLA Ops:
  0.6 2.1 %collective-permute-start.2 = (bf16[128,1024]{1,0:T(8,128)(2,1)}, bf16[128,1024]{1,0:T(8,128)(2,1)S(1)}, u32[]{:S(2)}, u32[]{:S(2)}) collective-permute-start(bf16[128,1024]{1,0:T(8,128)(2,1)} %refs_0_.1), channel_id=1, source_target_pairs={{0,32},{16,48},{32,64},{48,80},{64,96},{80,112},{96,0},{112,16},{1... | collective-permute-start | bytes 786440 | tf_op jit(solution)/shard_map/ppermute | solution.py:216
  2.7 2.2 %collective-permute-start.3 = (bf16[128,1024]{1,0:T(8,128)(2,1)}, bf16[128,1024]{1,0:T(8,128)(2,1)S(1)}, u32[]{:S(2)}, u32[]{:S(2)}) collective-permute-start(bf16[128,1024]{1,0:T(8,128)(2,1)} %refs_0_.1), channel_id=1, source_target_pairs={{0,96},{16,112},{32,0},{48,16},{64,32},{80,48},{96,64},{112,80},{1... | collective-permute-start | bytes 786440 | tf_op jit(solution)/shard_map/ppermute | solution.py:217
  4.9 1.0 %fusion = (bf16[64,1024]{1,0:T(8,128)(2,1)S(1)}, bf16[64,1024]{1,0:T(8,128)(2,1)S(1)}) fusion(bf16[128,1024]{1,0:T(8,128)(2,1)} %refs_0_.1), kind=kLoop, calls=%fused_computation.2 | loop fusion | bytes 524288 | tf_op jit(solution)/shard_map/slice | solution.py:215
  5.9 1.9 %collective-permute-start.1 = (bf16[64,1024]{1,0:T(8,128)(2,1)S(1)}, bf16[64,1024]{1,0:T(8,128)(2,1)S(1)}, u32[]{:S(2)}, u32[]{:S(2)}) collective-permute-start(bf16[64,1024]{1,0:T(8,128)(2,1)S(1)} %get-tuple-element.22), channel_id=1, source_target_pairs={{0,64},{16,80},{32,96},{48,112},{64,0},{80,16},{96,32},{112,48},{1... | collective-permute-start | bytes 393224 | tf_op jit(solution)/shard_map/ppermute | solution.py:215
  7.8 0.0 copy-start.2
  7.8 0.0 copy-start.3
  7.8 0.0 copy-start.6
  7.8 0.0 copy-start.9
  7.8 1.8 %collective-permute-start = (bf16[64,1024]{1,0:T(8,128)(2,1)S(1)}, bf16[64,1024]{1,0:T(8,128)(2,1)S(1)}, u32[]{:S(2)}, u32[]{:S(2)}) collective-permute-start(bf16[64,1024]{1,0:T(8,128)(2,1)S(1)} %get-tuple-element.23), channel_id=1, source_target_pairs={{0,64},{16,80},{32,96},{48,112},{64,0},{80,16},{96,32},{112,48},{1... | collective-permute-start | bytes 393224 | tf_op jit(solution)/shard_map/ppermute | solution.py:214
  9.6 0.0 collective-permute-start.4
  9.6 5.3 %shard_map.149.xt_ref = bf16[4,512,2048]{2,1,0:T(8,128)(2,1)S(1)} custom-call(bf16[4,2048,512]{2,1,0:T(8,128)(2,1)} %x_ref.3), custom_call_target="tpu_custom_call" | custom-call | bytes 16777216 | tf_op jit(solution)/shard_map/pallas_call | solution.py:41
  14.9 0.0 copy-start
  14.9 3.3 %copy-done = bf16[4,512,2048]{2,1,0:T(8,128)(2,1)} copy-done((bf16[4,512,2048]{2,1,0:T(8,128)(2,1)}, bf16[4,512,2048]{2,1,0:T(8,128)(2,1)S(1)}, u32[]{:S(2)}) %copy-start) | copy-done | bytes 8388632
  18.2 0.0 collective-permute-done.1.refs_4_
  18.2 0.0 collective-permute-done.refs_3_
  18.2 0.0 collective-permute-done.2.refs_1_
  18.2 0.0 collective-permute-done.3.refs_2_
  18.2 0.6 collective-permute-start.5
  18.8 0.1 collective-permute-start.6
  18.9 0.4 collective-permute-start.7
  19.3 0.1 collective-permute-start.8
  19.4 0.0 copy-done.14
  19.4 0.1 copy.16.refs_14_
  19.5 0.1 pad_add_fusion.pos_ref
  19.6 0.0 collective-permute-done.4.refs_5_
  19.6 0.9 %collective-permute-done.7.refs_8_ = bf16[64,1024]{1,0:T(8,128)(2,1)S(1)} collective-permute-done((bf16[64,1024]{1,0:T(8,128)(2,1)S(1)}, bf16[64,1024]{1,0:T(8,128)(2,1)S(1)}, u32[]{:S(2)}, u32[]{:S(2)}) %collective-permute-start.7) | collective-permute-done | bytes 131104 | tf_op jit(solution)/shard_map/ppermute | solution.py:221
  20.5 0.2 collective-permute-done.8.refs_9_
  20.7 0.0 collective-permute-done.5.refs_6_
  20.7 0.0 collective-permute-done.6.refs_7_
  20.7 0.0 copy-done.2
  20.7 0.0 copy-done.3
  20.7 0.0 copy-done.5
  20.8 0.0 copy-done.6
  20.8 0.0 copy-done.9
  20.8 0.0 slice-start.1
  20.8 0.0 copy-start.1
  20.8 0.0 copy-start.4
  20.8 0.0 copy-start.7
  20.8 0.0 copy-start.8
  20.8 0.0 copy-start.10
  20.8 0.0 copy-start.11
  20.9 0.0 copy-start.12
  20.9 0.0 copy-start.13
  20.9 10.5 %shard_map.150 = (f32[4,2048]{1,0:T(4,128)S(1)}, bf16[8,64,128]{2,1,0:T(8,128)(2,1)S(1)}) custom-call(s32[4,4]{1,0:T(4,128)S(1)} %copy-done.9, s32[3]{0:T(128)S(1)} %pad_add_fusion.pos_ref, bf16[128,1024]{1,0:T(8,128)(2,1)S(1)} %copy-done.3, bf16[128,1024]{1,0:T(8,128)(2,1)S(1)} %collective-permute-done.2.refs_1_, ...), custom_call_target="tpu_custom_call" | custom-call | flops 4294967296 | bytes 8388608 | tf_op jit(solution)/shard_map/pallas_call | solution.py:223
  31.4 9.2 %all_to_all.15.x_ref = bf16[8,64,128]{2,1,0:T(8,128)(2,1)S(1)} all-to-all(bf16[8,64,128]{2,1,0:T(8,128)(2,1)S(1)} %get-tuple-element.16), channel_id=1, replica_groups=mesh['mat'=8,'pts'=16] {'mat'}, dimensions={0} | all-to-all | bytes 262144 | tf_op jit(solution)/shard_map/all_to_all | solution.py:257
  40.6 15.5 %all_to_all.16.x_ref = bf16[16,64,128]{2,1,0:T(8,128)(2,1)S(1)} all-to-all(bf16[16,64,128]{2,1,0:T(8,128)(2,1)S(1)} %shard_map.151), channel_id=1, replica_groups=mesh['mat'=8,'pts'=16] {'pts'}, dimensions={0} | all-to-all | bytes 524288 | tf_op jit(solution)/shard_map/all_to_all | solution.py:258
  56.2 0.1 collective-permute-start.9
  56.3 1.2 %collective-permute-done.9.sum_ref_too = f32[64,128]{1,0:T(8,128)S(1)} collective-permute-done((f32[64,128]{1,0:T(8,128)S(1)}, f32[64,128]{1,0:T(8,128)S(1)}, u32[]{:S(2)}, u32[]{:S(2)}) %collective-permute-start.9) | collective-permute-done | bytes 32800 | tf_op jit(solution)/shard_map/ppermute | solution.py:259
  57.5 0.0 slice-done
  57.5 0.0 slice-done.1
  57.5 0.0 copy-done.1
  57.5 0.0 copy-done.4
  57.5 0.0 copy-done.7
  57.5 0.0 copy-done.8
  57.5 0.0 copy-done.10
  57.5 0.0 copy-done.11
  57.5 0.0 copy-done.12
  57.5 0.0 copy-done.13
  57.6 8.3 %shard_map.153 = (f32[4,8,128,128]{3,2,1,0:T(8,128)S(1)}, bf16[4,8,128,128]{3,2,1,0:T(8,128)(2,1)S(1)}, bf16[16,64]{1,0:T(8,128)(2,1)}) custom-call(s32[4,4]{1,0:T(4,128)S(1)} %copy-done.9, s32[3]{0:T(128)S(1)} %pad_add_fusion.pos_ref, f32[64,128]{1,0:T(8,128)S(1)} %shard_map.152.sum_ref, f32[64,128]{1,0:T(8,128)S(1)} %collective-permute-done.9.sum_ref_too, ...), custom_call_target="tpu_custom_call" | custom-call | flops 4294967296 | bytes 16777216 | tf_op jit(solution)/shard_map/pallas_call | solution.py:264
  65.9 0.2 collective-permute-start.10
  66.0 2.5 %collective-permute-done.10 = bf16[4,8,128,128]{3,2,1,0:T(8,128)(2,1)S(1)} collective-permute-done((bf16[4,8,128,128]{3,2,1,0:T(8,128)(2,1)S(1)}, bf16[4,8,128,128]{3,2,1,0:T(8,128)(2,1)S(1)}, u32[]{:S(2)}, u32[]{:S(2)}) %collective-permute-start.10) | collective-permute-done | bytes 1048608 | tf_op jit(solution)/shard_map/ppermute | solution.py:315
  68.5 0.3 add_convert_fusion
  68.8 23.6 %all_to_all.17.x_ref = bf16[64,64,128]{2,1,0:T(8,128)(2,1)S(1)} all-to-all(bf16[64,64,128]{2,1,0:T(8,128)(2,1)S(1)} %bitcast.21), channel_id=1, replica_groups={{0,1,2,3,4,5,6,7,8,9,10,11,12,13,14,15,32,33,34,35,36,37,38,39,40,41,42..., dimensions={0} | all-to-all | bytes 2097152 | tf_op jit(solution)/shard_map/all_to_all | solution.py:317
  92.4 0.8 shard_map.154
  (6 shorter events, 0.1 us)
Async XLA Ops:
  0.6 17.6 %collective-permute-start.2 = (bf16[128,1024]{1,0:T(8,128)(2,1)}, bf16[128,1024]{1,0:T(8,128)(2,1)S(1)}, u32[]{:S(2)}, u32[]{:S(2)}) collective-permute-start(bf16[128,1024]{1,0:T(8,128)(2,1)} %refs_0_.1), channel_id=1, source_target_pairs={{0,32},{16,48},{32,64},{48,80},{64,96},{80,112},{96,0},{112,16},{1... | collective-permute-start | bytes 786440 | tf_op jit(solution)/shard_map/ppermute | solution.py:216
  2.7 15.5 %collective-permute-start.3 = (bf16[128,1024]{1,0:T(8,128)(2,1)}, bf16[128,1024]{1,0:T(8,128)(2,1)S(1)}, u32[]{:S(2)}, u32[]{:S(2)}) collective-permute-start(bf16[128,1024]{1,0:T(8,128)(2,1)} %refs_0_.1), channel_id=1, source_target_pairs={{0,96},{16,112},{32,0},{48,16},{64,32},{80,48},{96,64},{112,80},{1... | collective-permute-start | bytes 786440 | tf_op jit(solution)/shard_map/ppermute | solution.py:217
  5.9 12.3 %collective-permute-start.1 = (bf16[64,1024]{1,0:T(8,128)(2,1)S(1)}, bf16[64,1024]{1,0:T(8,128)(2,1)S(1)}, u32[]{:S(2)}, u32[]{:S(2)}) collective-permute-start(bf16[64,1024]{1,0:T(8,128)(2,1)S(1)} %get-tuple-element.22), channel_id=1, source_target_pairs={{0,64},{16,80},{32,96},{48,112},{64,0},{80,16},{96,32},{112,48},{1... | collective-permute-start | bytes 393224 | tf_op jit(solution)/shard_map/ppermute | solution.py:215
  7.8 11.6 %copy-start.14 = (f32[64]{0:T(128)S(1)}, f32[64]{0:T(128)}, u32[]{:S(2)}) copy-start(f32[64]{0:T(128)} %param.20) | copy-start | bytes 772
  7.8 13.0 %copy-start.2 = (bf16[4,2048,64]{1,2,0:T(8,128)(2,1)S(1)}, bf16[4,2048,64]{1,2,0:T(8,128)(2,1)}, u32[]{:S(2)}) copy-start(bf16[4,2048,64]{1,2,0:T(8,128)(2,1)} %param.17) | copy-start | bytes 3145732
  7.8 13.0 %copy-start.3 = (bf16[128,1024]{1,0:T(8,128)(2,1)S(1)}, bf16[128,1024]{1,0:T(8,128)(2,1)}, u32[]{:S(2)}) copy-start(bf16[128,1024]{1,0:T(8,128)(2,1)} %refs_0_.1) | copy-start | bytes 786436
  7.8 13.0 %copy-start.5 = (f32[4,2048]{1,0:T(4,128)S(1)}, f32[4,2048]{1,0:T(4,128)}, u32[]{:S(2)}) copy-start(f32[4,2048]{1,0:T(4,128)} %w_ref.1) | copy-start | bytes 98308
  7.8 13.0 %copy-start.6 = (s32[4,2048]{1,0:T(4,128)S(1)}, s32[4,2048]{1,0:T(4,128)}, u32[]{:S(2)}) copy-start(s32[4,2048]{1,0:T(4,128)} %ids_ref.1) | copy-start | bytes 98308
  7.8 13.0 %copy-start.9 = (s32[4,4]{1,0:T(4,128)S(1)}, s32[4,4]{1,0:T(4,128)}, u32[]{:S(2)}) copy-start(s32[4,4]{1,0:T(4,128)} %tid_ref.3) | copy-start | bytes 196
  7.8 10.4 %collective-permute-start = (bf16[64,1024]{1,0:T(8,128)(2,1)S(1)}, bf16[64,1024]{1,0:T(8,128)(2,1)S(1)}, u32[]{:S(2)}, u32[]{:S(2)}) collective-permute-start(bf16[64,1024]{1,0:T(8,128)(2,1)S(1)} %get-tuple-element.23), channel_id=1, source_target_pairs={{0,64},{16,80},{32,96},{48,112},{64,0},{80,16},{96,32},{112,48},{1... | collective-permute-start | bytes 393224 | tf_op jit(solution)/shard_map/ppermute | solution.py:214
  9.6 10.0 %collective-permute-start.4 = (bf16[128,1024]{1,0:T(8,128)(2,1)}, bf16[128,1024]{1,0:T(8,128)(2,1)S(1)}, u32[]{:S(2)}, u32[]{:S(2)}) collective-permute-start(bf16[128,1024]{1,0:T(8,128)(2,1)} %refs_0_.1), channel_id=1, source_target_pairs={{0,16},{16,0},{32,48},{48,32},{64,80},{80,64},{96,112},{112,96},{1... | collective-permute-start | bytes 786440 | tf_op jit(solution)/shard_map/ppermute | solution.py:221
  14.9 3.3 %copy-start = (bf16[4,512,2048]{2,1,0:T(8,128)(2,1)}, bf16[4,512,2048]{2,1,0:T(8,128)(2,1)S(1)}, u32[]{:S(2)}) copy-start(bf16[4,512,2048]{2,1,0:T(8,128)(2,1)S(1)} %shard_map.149.xt_ref) | copy-start | bytes 25165828
  18.2 2.5 %collective-permute-start.5 = (bf16[128,1024]{1,0:T(8,128)(2,1)S(1)}, bf16[128,1024]{1,0:T(8,128)(2,1)S(1)}, u32[]{:S(2)}, u32[]{:S(2)}) collective-permute-start(bf16[128,1024]{1,0:T(8,128)(2,1)S(1)} %collective-permute-done.2.refs_1_), channel_id=1, source_target_pairs={{0,16},{16,0},{32,48},{48,32},{64,80},{80,64},{96,112},{112,96},{1... | collective-permute-start | bytes 786440 | tf_op jit(solution)/shard_map/ppermute | solution.py:221
  18.8 1.9 %collective-permute-start.6 = (bf16[128,1024]{1,0:T(8,128)(2,1)S(1)}, bf16[128,1024]{1,0:T(8,128)(2,1)S(1)}, u32[]{:S(2)}, u32[]{:S(2)}) collective-permute-start(bf16[128,1024]{1,0:T(8,128)(2,1)S(1)} %collective-permute-done.3.refs_2_), channel_id=1, source_target_pairs={{0,16},{16,0},{32,48},{48,32},{64,80},{80,64},{96,112},{112,96},{1... | collective-permute-start | bytes 786440 | tf_op jit(solution)/shard_map/ppermute | solution.py:221
  18.9 1.6 %collective-permute-start.7 = (bf16[64,1024]{1,0:T(8,128)(2,1)S(1)}, bf16[64,1024]{1,0:T(8,128)(2,1)S(1)}, u32[]{:S(2)}, u32[]{:S(2)}) collective-permute-start(bf16[64,1024]{1,0:T(8,128)(2,1)S(1)} %collective-permute-done.refs_3_), channel_id=1, source_target_pairs={{0,16},{16,0},{32,48},{48,32},{64,80},{80,64},{96,112},{112,96},{1... | collective-permute-start | bytes 393224 | tf_op jit(solution)/shard_map/ppermute | solution.py:221
  19.3 1.4 %collective-permute-start.8 = (bf16[64,1024]{1,0:T(8,128)(2,1)S(1)}, bf16[64,1024]{1,0:T(8,128)(2,1)S(1)}, u32[]{:S(2)}, u32[]{:S(2)}) collective-permute-start(bf16[64,1024]{1,0:T(8,128)(2,1)S(1)} %collective-permute-done.1.refs_4_), channel_id=1, source_target_pairs={{0,16},{16,0},{32,48},{48,32},{64,80},{80,64},{96,112},{112,96},{1... | collective-permute-start | bytes 393224 | tf_op jit(solution)/shard_map/ppermute | solution.py:221
  20.7 36.8 %slice-start = ((s8[8388608]{0:T(1024)(128)(4,1)}), s8[4194304]{0:T(1024)(128)(4,1)S(1)}, s32[]{:S(2)}) async-start(s8[8388608]{0:T(1024)(128)(4,1)} %bitcast.12), calls=%async_computation.3 | async-start | bytes 8388608
  20.8 36.7 %slice-start.1 = ((s8[8388608]{0:T(1024)(128)(4,1)}), s8[4194304]{0:T(1024)(128)(4,1)S(1)}, s32[]{:S(2)}) async-start(s8[8388608]{0:T(1024)(128)(4,1)} %bitcast.12), calls=%async_computation.4 | async-start | bytes 8388608
  20.8 36.7 %copy-start.1 = (bf16[4,512,2048]{2,1,0:T(8,128)(2,1)S(1)}, bf16[4,512,2048]{2,1,0:T(8,128)(2,1)}, u32[]{:S(2)}) copy-start(bf16[4,512,2048]{2,1,0:T(8,128)(2,1)} %copy-done) | copy-start | bytes 25165828
  20.8 36.7 %copy-start.4 = (bf16[256,256]{1,0:T(8,128)(2,1)S(1)}, bf16[256,256]{1,0:T(8,128)(2,1)}, u32[]{:S(2)}) copy-start(bf16[256,256]{1,0:T(8,128)(2,1)} %w2_ref.1) | copy-start | bytes 393220
  20.8 36.7 %copy-start.7 = (bf16[64,256]{1,0:T(8,128)(2,1)S(1)}, bf16[64,256]{1,0:T(8,128)(2,1)}, u32[]{:S(2)}) copy-start(bf16[64,256]{1,0:T(8,128)(2,1)} %w1_ref.1) | copy-start | bytes 98308
  20.8 36.7 %copy-start.8 = (bf16[256,64]{0,1:T(8,128)(2,1)S(1)}, bf16[256,64]{0,1:T(8,128)(2,1)}, u32[]{:S(2)}) copy-start(bf16[256,64]{0,1:T(8,128)(2,1)} %param.26) | copy-start | bytes 98308
  20.8 36.7 %copy-start.10 = (f32[256]{0:T(256)S(1)}, f32[256]{0:T(256)}, u32[]{:S(2)}) copy-start(f32[256]{0:T(256)} %param.23) | copy-start | bytes 3076
  20.8 36.7 %copy-start.11 = (f32[256]{0:T(256)S(1)}, f32[256]{0:T(256)}, u32[]{:S(2)}) copy-start(f32[256]{0:T(256)} %param.25) | copy-start | bytes 3076
  20.9 36.7 %copy-start.12 = (f32[64]{0:T(128)S(1)}, f32[64]{0:T(128)}, u32[]{:S(2)}) copy-start(f32[64]{0:T(128)} %param.21) | copy-start | bytes 772
  20.9 36.7 %copy-start.13 = (f32[64]{0:T(128)S(1)}, f32[64]{0:T(128)}, u32[]{:S(2)}) copy-start(f32[64]{0:T(128)} %param.27) | copy-start | bytes 772
  56.2 1.3 %collective-permute-start.9 = (f32[64,128]{1,0:T(8,128)S(1)}, f32[64,128]{1,0:T(8,128)S(1)}, u32[]{:S(2)}, u32[]{:S(2)}) collective-permute-start(f32[64,128]{1,0:T(8,128)S(1)} %shard_map.152.sum_ref), channel_id=1, source_target_pairs={{0,16},{16,0},{32,48},{48,32},{64,80},{80,64},{96,112},{112,96},{1... | collective-permute-start | bytes 98312 | tf_op jit(solution)/shard_map/ppermute | solution.py:259
  65.9 2.7 %collective-permute-start.10 = (bf16[4,8,128,128]{3,2,1,0:T(8,128)(2,1)S(1)}, bf16[4,8,128,128]{3,2,1,0:T(8,128)(2,1)S(1)}, u32[]{:S(2)}, u32[]{:S(2)}) collective-permute-start(bf16[4,8,128,128]{3,2,1,0:T(8,128)(2,1)S(1)} %get-tuple-element.20), channel_id=1, source_target_pairs={{0,16},{16,0},{32,48},{48,32},{64,80},{80,64},{96,112},{112,96},{1... | collective-permute-start | bytes 3145736 | tf_op jit(solution)/shard_map/ppermute | solution.py:315

commit v4 on v3

--- a/solution.py
+++ b/solution.py
@@ -43,7 +43,7 @@
         grid=(batches, points // chunk),
         in_specs=[pl.BlockSpec((1, chunk, orbitals), lambda b, r: (b, r, 0))],
         out_specs=pl.BlockSpec((1, orbitals, chunk), lambda b, r: (b, 0, r)),
-        out_shape=jax.ShapeDtypeStruct((batches, orbitals, points), x.dtype),
+        out_shape=pltpu.HBM((batches, orbitals, points), x.dtype),
         compiler_params=pltpu.CompilerParams(vmem_limit_bytes=16 * MB),
         cost_estimate=pl.CostEstimate(
             flops=0, bytes_accessed=4 * x.size, transcendentals=0
@@ -221,7 +221,7 @@
     slabs += [lax.ppermute(slab, "mat", swap) for slab in slabs]
 
     density, partial = pl.pallas_call(
-        functools.partial(density_kernel, tile, chunk, chips),
+        functools.partial(density_kernel, tile, points, chips),
         grid_spec=pltpu.PrefetchScalarGridSpec(
             num_scalar_prefetch=2,
             grid=(batches,),

time: 93.5 us -> 93.1 us (level)
  local copies, waits for them, and re-layouts: 4.43 us -> 1.17 us
  Pallas kernels: 25 us -> 27.8 us
    unnamed x34 -> x32, local copies, waits for them, and re-layouts: 3.34 us -> 0.08 us
    pallas_call x1, Pallas kernels: 5.29 us -> 8.04 us  [transposed(): pl.pallas_call(transpose_kernel, grid=(batches, points // chunk), in_spec...]
  transfers between devices with their start and end apart: 11 -> 11, of which waited for: 4 -> 5; matrix products, arithmetic and copies ran while one was open for 1% -> 1% of each run, Pallas kernels for 6% -> 9%
where the time goes in v4:
time: 93.1 us; the launch traced here: 92.9 us
  blocking collectives  48.2 us (52%)
  Pallas kernels  27.8 us (30%)
  starting transfers between devices  9.23 us (10%)
  waiting for transfers between devices  5.26 us (6%)
  local copies, waits for them, and re-layouts  1.17 us (1%)
    all_to_all x1, blocking collectives, shards(): lax.all_to_all(joined, ('mat', 'pts'), 0, 0, tiled=True, axis_index_group...  23.6 us
    all_to_all x1, blocking collectives, shards(): mine_sum = summed(lax.all_to_all(first, 'pts', 0, 0, tiled=True), kind=F32)  15.5 us
    pallas_call x1, Pallas kernels, shards(): pl.pallas_call(functools.partial(density_kernel, tile, points, chips), gr...  10.6 us
    all_to_all x1, blocking collectives, shards(): first = summed(lax.all_to_all(partial, 'mat', 0, 0, tiled=True), (columns,))  9.04 us
    pallas_call x1, Pallas kernels, shards(): pl.pallas_call(functools.partial(potential_kernel, tile, chunk, factor),...  8.3 us
    pallas_call x1, Pallas kernels, transposed(): pl.pallas_call(transpose_kernel, grid=(batches, points // chunk), in_spec...  8.04 us
    ppermute x1, waiting for transfers between devices, shards(): joined = (own + lax.ppermute(other, 'mat', swap).astype(F32)).astype(BF)  2.5 us
    ppermute x1, starting transfers between devices, shards(): above = lax.ppermute(density_matrix, 'mat', down)  2.2 us
  transfers between devices with their start and end apart: 11, of which 5 were waited for; matrix products, arithmetic and copies ran while one was open for 1% of the time, Pallas kernels for 9%

profile of v4, /device:TPU:0, one launch (start us, length us, event | category | flops | bytes accessed | tf_op | source)
XLA Modules:
  0.0 92.9 jit_solution(14228372302944798340)
XLA Ops:
  0.6 2.1 %collective-permute-start.2 = (bf16[128,1024]{1,0:T(8,128)(2,1)}, bf16[128,1024]{1,0:T(8,128)(2,1)S(1)}, u32[]{:S(2)}, u32[]{:S(2)}) collective-permute-start(bf16[128,1024]{1,0:T(8,128)(2,1)} %refs_0_.1), channel_id=1, source_target_pairs={{0,32},{16,48},{32,64},{48,80},{64,96},{80,112},{96,0},{112,16},{1... | collective-permute-start | bytes 786440 | tf_op jit(solution)/shard_map/ppermute | solution.py:216
  2.7 2.2 %collective-permute-start.3 = (bf16[128,1024]{1,0:T(8,128)(2,1)}, bf16[128,1024]{1,0:T(8,128)(2,1)S(1)}, u32[]{:S(2)}, u32[]{:S(2)}) collective-permute-start(bf16[128,1024]{1,0:T(8,128)(2,1)} %refs_0_.1), channel_id=1, source_target_pairs={{0,96},{16,112},{32,0},{48,16},{64,32},{80,48},{96,64},{112,80},{1... | collective-permute-start | bytes 786440 | tf_op jit(solution)/shard_map/ppermute | solution.py:217
  4.9 1.0 %fusion = (bf16[64,1024]{1,0:T(8,128)(2,1)S(1)}, bf16[64,1024]{1,0:T(8,128)(2,1)S(1)}) fusion(bf16[128,1024]{1,0:T(8,128)(2,1)} %refs_0_.1), kind=kLoop, calls=%fused_computation.2 | loop fusion | bytes 524288 | tf_op jit(solution)/shard_map/slice | solution.py:215
  5.9 1.9 %collective-permute-start.1 = (bf16[64,1024]{1,0:T(8,128)(2,1)S(1)}, bf16[64,1024]{1,0:T(8,128)(2,1)S(1)}, u32[]{:S(2)}, u32[]{:S(2)}) collective-permute-start(bf16[64,1024]{1,0:T(8,128)(2,1)S(1)} %get-tuple-element.22), channel_id=1, source_target_pairs={{0,64},{16,80},{32,96},{48,112},{64,0},{80,16},{96,32},{112,48},{1... | collective-permute-start | bytes 393224 | tf_op jit(solution)/shard_map/ppermute | solution.py:215
  7.8 0.0 copy-start.1
  7.8 0.0 copy-start.2
  7.8 0.0 copy-start.4
  7.8 0.0 copy-start.5
  7.8 0.0 copy-start.8
  7.8 1.8 %collective-permute-start = (bf16[64,1024]{1,0:T(8,128)(2,1)S(1)}, bf16[64,1024]{1,0:T(8,128)(2,1)S(1)}, u32[]{:S(2)}, u32[]{:S(2)}) collective-permute-start(bf16[64,1024]{1,0:T(8,128)(2,1)S(1)} %get-tuple-element.23), channel_id=1, source_target_pairs={{0,64},{16,80},{32,96},{48,112},{64,0},{80,16},{96,32},{112,48},{1... | collective-permute-start | bytes 393224 | tf_op jit(solution)/shard_map/ppermute | solution.py:214
  9.6 0.0 collective-permute-start.4
  9.6 8.0 %shard_map.149.xt_ref = bf16[4,512,2048]{2,1,0:T(8,128)(2,1)} custom-call(bf16[4,2048,512]{2,1,0:T(8,128)(2,1)} %x_ref.3), custom_call_target="tpu_custom_call" | custom-call | bytes 16777216 | tf_op jit(solution)/shard_map/pallas_call | solution.py:41
  17.7 0.0 collective-permute-done.1.refs_4_
  17.7 0.5 collective-permute-done.refs_3_
  18.1 0.0 collective-permute-done.2.refs_1_
  18.1 0.0 collective-permute-done.3.refs_2_
  18.1 0.1 collective-permute-start.5
  18.3 0.4 collective-permute-start.6
  18.6 0.1 collective-permute-start.7
  18.8 0.4 collective-permute-start.8
  19.2 0.0 copy-done.13
  19.2 0.1 copy.16.refs_14_
  19.3 0.1 pad_add_fusion.pos_ref
  19.3 0.0 collective-permute-done.4.refs_5_
  19.3 0.9 collective-permute-done.7.refs_8_
  20.2 0.2 collective-permute-done.8.refs_9_
  20.4 0.0 collective-permute-done.5.refs_6_
  20.4 0.0 collective-permute-done.6.refs_7_
  20.4 0.0 slice-start
  20.4 0.0 copy-done.1
  20.4 0.0 copy-done.2
  20.5 0.0 copy-done.4
  20.5 0.0 copy-done.5
  20.5 0.0 copy-done.8
  20.5 0.0 slice-start.1
  20.5 0.0 copy-start
  20.5 0.0 copy-start.3
  20.5 0.0 copy-start.6
  20.5 0.0 copy-start.7
  20.5 0.0 copy-start.9
  20.6 0.0 copy-start.10
  20.6 0.0 copy-start.11
  20.6 0.0 copy-start.12
  20.6 10.6 %shard_map.150 = (f32[4,2048]{1,0:T(4,128)S(1)}, bf16[8,64,128]{2,1,0:T(8,128)(2,1)S(1)}) custom-call(s32[4,4]{1,0:T(4,128)S(1)} %copy-done.8, s32[3]{0:T(128)S(1)} %pad_add_fusion.pos_ref, bf16[128,1024]{1,0:T(8,128)(2,1)S(1)} %copy-done.2, bf16[128,1024]{1,0:T(8,128)(2,1)S(1)} %collective-permute-done.2.refs_1_, ...), custom_call_target="tpu_custom_call" | custom-call | flops 4294967296 | bytes 8388608 | tf_op jit(solution)/shard_map/pallas_call | solution.py:223
  31.2 9.0 %all_to_all.15.x_ref = bf16[8,64,128]{2,1,0:T(8,128)(2,1)S(1)} all-to-all(bf16[8,64,128]{2,1,0:T(8,128)(2,1)S(1)} %get-tuple-element.16), channel_id=1, replica_groups=mesh['mat'=8,'pts'=16] {'mat'}, dimensions={0} | all-to-all | bytes 262144 | tf_op jit(solution)/shard_map/all_to_all | solution.py:257
  40.3 15.5 %all_to_all.16.x_ref = bf16[16,64,128]{2,1,0:T(8,128)(2,1)S(1)} all-to-all(bf16[16,64,128]{2,1,0:T(8,128)(2,1)S(1)} %shard_map.151), channel_id=1, replica_groups=mesh['mat'=8,'pts'=16] {'pts'}, dimensions={0} | all-to-all | bytes 524288 | tf_op jit(solution)/shard_map/all_to_all | solution.py:258
  55.9 0.1 collective-permute-start.9
  55.9 1.2 %collective-permute-done.9.sum_ref_too = f32[64,128]{1,0:T(8,128)S(1)} collective-permute-done((f32[64,128]{1,0:T(8,128)S(1)}, f32[64,128]{1,0:T(8,128)S(1)}, u32[]{:S(2)}, u32[]{:S(2)}) %collective-permute-start.9) | collective-permute-done | bytes 32800 | tf_op jit(solution)/shard_map/ppermute | solution.py:259
  57.1 0.0 slice-done
  57.1 0.0 slice-done.1
  57.1 0.0 copy-done
  57.1 0.0 copy-done.3
  57.2 0.0 copy-done.6
  57.2 0.0 copy-done.7
  57.2 0.0 copy-done.9
  57.2 0.0 copy-done.10
  57.2 0.0 copy-done.11
  57.2 0.0 copy-done.12
  57.2 8.3 %shard_map.153 = (f32[4,8,128,128]{3,2,1,0:T(8,128)S(1)}, bf16[4,8,128,128]{3,2,1,0:T(8,128)(2,1)S(1)}, bf16[16,64]{1,0:T(8,128)(2,1)}) custom-call(s32[4,4]{1,0:T(4,128)S(1)} %copy-done.8, s32[3]{0:T(128)S(1)} %pad_add_fusion.pos_ref, f32[64,128]{1,0:T(8,128)S(1)} %shard_map.152.sum_ref, f32[64,128]{1,0:T(8,128)S(1)} %collective-permute-done.9.sum_ref_too, ...), custom_call_target="tpu_custom_call" | custom-call | flops 4294967296 | bytes 16777216 | tf_op jit(solution)/shard_map/pallas_call | solution.py:264
  65.5 0.2 collective-permute-start.10
  65.7 2.5 %collective-permute-done.10 = bf16[4,8,128,128]{3,2,1,0:T(8,128)(2,1)S(1)} collective-permute-done((bf16[4,8,128,128]{3,2,1,0:T(8,128)(2,1)S(1)}, bf16[4,8,128,128]{3,2,1,0:T(8,128)(2,1)S(1)}, u32[]{:S(2)}, u32[]{:S(2)}) %collective-permute-start.10) | collective-permute-done | bytes 1048608 | tf_op jit(solution)/shard_map/ppermute | solution.py:315
  68.2 0.3 add_convert_fusion
  68.5 23.6 %all_to_all.17.x_ref = bf16[64,64,128]{2,1,0:T(8,128)(2,1)S(1)} all-to-all(bf16[64,64,128]{2,1,0:T(8,128)(2,1)S(1)} %bitcast.21), channel_id=1, replica_groups={{0,1,2,3,4,5,6,7,8,9,10,11,12,13,14,15,32,33,34,35,36,37,38,39,40,41,42..., dimensions={0} | all-to-all | bytes 2097152 | tf_op jit(solution)/shard_map/all_to_all | solution.py:317
  92.1 0.8 shard_map.154
  (4 shorter events, 0.1 us)
Async XLA Ops:
  0.6 17.5 %collective-permute-start.2 = (bf16[128,1024]{1,0:T(8,128)(2,1)}, bf16[128,1024]{1,0:T(8,128)(2,1)S(1)}, u32[]{:S(2)}, u32[]{:S(2)}) collective-permute-start(bf16[128,1024]{1,0:T(8,128)(2,1)} %refs_0_.1), channel_id=1, source_target_pairs={{0,32},{16,48},{32,64},{48,80},{64,96},{80,112},{96,0},{112,16},{1... | collective-permute-start | bytes 786440 | tf_op jit(solution)/shard_map/ppermute | solution.py:216
  2.7 15.4 %collective-permute-start.3 = (bf16[128,1024]{1,0:T(8,128)(2,1)}, bf16[128,1024]{1,0:T(8,128)(2,1)S(1)}, u32[]{:S(2)}, u32[]{:S(2)}) collective-permute-start(bf16[128,1024]{1,0:T(8,128)(2,1)} %refs_0_.1), channel_id=1, source_target_pairs={{0,96},{16,112},{32,0},{48,16},{64,32},{80,48},{96,64},{112,80},{1... | collective-permute-start | bytes 786440 | tf_op jit(solution)/shard_map/ppermute | solution.py:217
  5.9 11.8 %collective-permute-start.1 = (bf16[64,1024]{1,0:T(8,128)(2,1)S(1)}, bf16[64,1024]{1,0:T(8,128)(2,1)S(1)}, u32[]{:S(2)}, u32[]{:S(2)}) collective-permute-start(bf16[64,1024]{1,0:T(8,128)(2,1)S(1)} %get-tuple-element.22), channel_id=1, source_target_pairs={{0,64},{16,80},{32,96},{48,112},{64,0},{80,16},{96,32},{112,48},{1... | collective-permute-start | bytes 393224 | tf_op jit(solution)/shard_map/ppermute | solution.py:215
  7.8 11.4 %copy-start.13 = (f32[64]{0:T(128)S(1)}, f32[64]{0:T(128)}, u32[]{:S(2)}) copy-start(f32[64]{0:T(128)} %param.20) | copy-start | bytes 772
  7.8 12.7 %copy-start.1 = (bf16[4,2048,64]{1,2,0:T(8,128)(2,1)S(1)}, bf16[4,2048,64]{1,2,0:T(8,128)(2,1)}, u32[]{:S(2)}) copy-start(bf16[4,2048,64]{1,2,0:T(8,128)(2,1)} %param.17) | copy-start | bytes 3145732
  7.8 12.7 %copy-start.2 = (bf16[128,1024]{1,0:T(8,128)(2,1)S(1)}, bf16[128,1024]{1,0:T(8,128)(2,1)}, u32[]{:S(2)}) copy-start(bf16[128,1024]{1,0:T(8,128)(2,1)} %refs_0_.1) | copy-start | bytes 786436
  7.8 12.7 %copy-start.4 = (f32[4,2048]{1,0:T(4,128)S(1)}, f32[4,2048]{1,0:T(4,128)}, u32[]{:S(2)}) copy-start(f32[4,2048]{1,0:T(4,128)} %w_ref.1) | copy-start | bytes 98308
  7.8 12.7 %copy-start.5 = (s32[4,2048]{1,0:T(4,128)S(1)}, s32[4,2048]{1,0:T(4,128)}, u32[]{:S(2)}) copy-start(s32[4,2048]{1,0:T(4,128)} %ids_ref.1) | copy-start | bytes 98308
  7.8 12.7 %copy-start.8 = (s32[4,4]{1,0:T(4,128)S(1)}, s32[4,4]{1,0:T(4,128)}, u32[]{:S(2)}) copy-start(s32[4,4]{1,0:T(4,128)} %tid_ref.3) | copy-start | bytes 196
  7.8 10.3 %collective-permute-start = (bf16[64,1024]{1,0:T(8,128)(2,1)S(1)}, bf16[64,1024]{1,0:T(8,128)(2,1)S(1)}, u32[]{:S(2)}, u32[]{:S(2)}) collective-permute-start(bf16[64,1024]{1,0:T(8,128)(2,1)S(1)} %get-tuple-element.23), channel_id=1, source_target_pairs={{0,64},{16,80},{32,96},{48,112},{64,0},{80,16},{96,32},{112,48},{1... | collective-permute-start | bytes 393224 | tf_op jit(solution)/shard_map/ppermute | solution.py:214
  9.6 9.7 %collective-permute-start.4 = (bf16[128,1024]{1,0:T(8,128)(2,1)}, bf16[128,1024]{1,0:T(8,128)(2,1)S(1)}, u32[]{:S(2)}, u32[]{:S(2)}) collective-permute-start(bf16[128,1024]{1,0:T(8,128)(2,1)} %refs_0_.1), channel_id=1, source_target_pairs={{0,16},{16,0},{32,48},{48,32},{64,80},{80,64},{96,112},{112,96},{1... | collective-permute-start | bytes 786440 | tf_op jit(solution)/shard_map/ppermute | solution.py:221
  18.1 2.3 %collective-permute-start.5 = (bf16[128,1024]{1,0:T(8,128)(2,1)S(1)}, bf16[128,1024]{1,0:T(8,128)(2,1)S(1)}, u32[]{:S(2)}, u32[]{:S(2)}) collective-permute-start(bf16[128,1024]{1,0:T(8,128)(2,1)S(1)} %collective-permute-done.2.refs_1_), channel_id=1, source_target_pairs={{0,16},{16,0},{32,48},{48,32},{64,80},{80,64},{96,112},{112,96},{1... | collective-permute-start | bytes 786440 | tf_op jit(solution)/shard_map/ppermute | solution.py:221
  18.3 2.2 %collective-permute-start.6 = (bf16[128,1024]{1,0:T(8,128)(2,1)S(1)}, bf16[128,1024]{1,0:T(8,128)(2,1)S(1)}, u32[]{:S(2)}, u32[]{:S(2)}) collective-permute-start(bf16[128,1024]{1,0:T(8,128)(2,1)S(1)} %collective-permute-done.3.refs_2_), channel_id=1, source_target_pairs={{0,16},{16,0},{32,48},{48,32},{64,80},{80,64},{96,112},{112,96},{1... | collective-permute-start | bytes 786440 | tf_op jit(solution)/shard_map/ppermute | solution.py:221
  18.6 1.6 %collective-permute-start.7 = (bf16[64,1024]{1,0:T(8,128)(2,1)S(1)}, bf16[64,1024]{1,0:T(8,128)(2,1)S(1)}, u32[]{:S(2)}, u32[]{:S(2)}) collective-permute-start(bf16[64,1024]{1,0:T(8,128)(2,1)S(1)} %collective-permute-done.refs_3_), channel_id=1, source_target_pairs={{0,16},{16,0},{32,48},{48,32},{64,80},{80,64},{96,112},{112,96},{1... | collective-permute-start | bytes 393224 | tf_op jit(solution)/shard_map/ppermute | solution.py:221
  18.8 1.6 %collective-permute-start.8 = (bf16[64,1024]{1,0:T(8,128)(2,1)S(1)}, bf16[64,1024]{1,0:T(8,128)(2,1)S(1)}, u32[]{:S(2)}, u32[]{:S(2)}) collective-permute-start(bf16[64,1024]{1,0:T(8,128)(2,1)S(1)} %collective-permute-done.1.refs_4_), channel_id=1, source_target_pairs={{0,16},{16,0},{32,48},{48,32},{64,80},{80,64},{96,112},{112,96},{1... | collective-permute-start | bytes 393224 | tf_op jit(solution)/shard_map/ppermute | solution.py:221
  20.4 36.7 %slice-start = ((s8[8388608]{0:T(1024)(128)(4,1)}), s8[4194304]{0:T(1024)(128)(4,1)S(1)}, s32[]{:S(2)}) async-start(s8[8388608]{0:T(1024)(128)(4,1)} %bitcast.12), calls=%async_computation.3 | async-start | bytes 8388608
  20.5 36.7 %slice-start.1 = ((s8[8388608]{0:T(1024)(128)(4,1)}), s8[4194304]{0:T(1024)(128)(4,1)S(1)}, s32[]{:S(2)}) async-start(s8[8388608]{0:T(1024)(128)(4,1)} %bitcast.12), calls=%async_computation.4 | async-start | bytes 8388608
  20.5 36.7 %copy-start = (bf16[4,512,2048]{2,1,0:T(8,128)(2,1)S(1)}, bf16[4,512,2048]{2,1,0:T(8,128)(2,1)}, u32[]{:S(2)}) copy-start(bf16[4,512,2048]{2,1,0:T(8,128)(2,1)} %shard_map.149.xt_ref) | copy-start | bytes 25165828
  20.5 36.6 %copy-start.3 = (bf16[256,256]{1,0:T(8,128)(2,1)S(1)}, bf16[256,256]{1,0:T(8,128)(2,1)}, u32[]{:S(2)}) copy-start(bf16[256,256]{1,0:T(8,128)(2,1)} %w2_ref.1) | copy-start | bytes 393220
  20.5 36.6 %copy-start.6 = (bf16[64,256]{1,0:T(8,128)(2,1)S(1)}, bf16[64,256]{1,0:T(8,128)(2,1)}, u32[]{:S(2)}) copy-start(bf16[64,256]{1,0:T(8,128)(2,1)} %w1_ref.1) | copy-start | bytes 98308
  20.5 36.6 %copy-start.7 = (bf16[256,64]{0,1:T(8,128)(2,1)S(1)}, bf16[256,64]{0,1:T(8,128)(2,1)}, u32[]{:S(2)}) copy-start(bf16[256,64]{0,1:T(8,128)(2,1)} %param.26) | copy-start | bytes 98308
  20.5 36.6 %copy-start.9 = (f32[256]{0:T(256)S(1)}, f32[256]{0:T(256)}, u32[]{:S(2)}) copy-start(f32[256]{0:T(256)} %param.23) | copy-start | bytes 3076
  20.6 36.6 %copy-start.10 = (f32[256]{0:T(256)S(1)}, f32[256]{0:T(256)}, u32[]{:S(2)}) copy-start(f32[256]{0:T(256)} %param.25) | copy-start | bytes 3076
  20.6 36.6 %copy-start.11 = (f32[64]{0:T(128)S(1)}, f32[64]{0:T(128)}, u32[]{:S(2)}) copy-start(f32[64]{0:T(128)} %param.21) | copy-start | bytes 772
  20.6 36.6 %copy-start.12 = (f32[64]{0:T(128)S(1)}, f32[64]{0:T(128)}, u32[]{:S(2)}) copy-start(f32[64]{0:T(128)} %param.27) | copy-start | bytes 772
  55.9 1.3 %collective-permute-start.9 = (f32[64,128]{1,0:T(8,128)S(1)}, f32[64,128]{1,0:T(8,128)S(1)}, u32[]{:S(2)}, u32[]{:S(2)}) collective-permute-start(f32[64,128]{1,0:T(8,128)S(1)} %shard_map.152.sum_ref), channel_id=1, source_target_pairs={{0,16},{16,0},{32,48},{48,32},{64,80},{80,64},{96,112},{112,96},{1... | collective-permute-start | bytes 98312 | tf_op jit(solution)/shard_map/ppermute | solution.py:259
  65.5 2.7 %collective-permute-start.10 = (bf16[4,8,128,128]{3,2,1,0:T(8,128)(2,1)S(1)}, bf16[4,8,128,128]{3,2,1,0:T(8,128)(2,1)S(1)}, u32[]{:S(2)}, u32[]{:S(2)}) collective-permute-start(bf16[4,8,128,128]{3,2,1,0:T(8,128)(2,1)S(1)} %get-tuple-element.20), channel_id=1, source_target_pairs={{0,16},{16,0},{32,48},{48,32},{64,80},{80,64},{96,112},{112,96},{1... | collective-permute-start | bytes 3145736 | tf_op jit(solution)/shard_map/ppermute | solution.py:315
